TPU v7x, 128 devices: a whole 4x4x4 slice. The times are simulated.
128 devices in a mesh: req: 64 (over y, z_hi, x, core), tp: 2 (over z_lo).
Axes of the slice: x: 4, y: 4, z: 4 (z_hi: 2, z_lo: 2; z = z_hi * 2 + z_lo), core: 2. Of those that a mesh axis runs over, the one named last changes fastest.
Arguments:
- tokens: bfloat16 [32768, 2048], P('req', 'tp'), may hold values from -6 to 6
- attn_gain: float32 [2048], replicated, may hold values from 0.1 to 1.9
- w_query: bfloat16 [2048, 1024], P(None, 'tp'), may hold values from -0.25 to 0.25
- key_weight: bfloat16 [2048, 256], P(None, 'tp'), may hold values from -0.125 to 0.125
- value_weight: bfloat16 [2048, 256], P(None, 'tp'), may hold values from -0.125 to 0.125
- w_attn_out: bfloat16 [1024, 2048], P('tp'), may hold values from -1 to 1
- kv_pages: bfloat16 [4096, 2, 2, 128, 128], P('req', None, 'tp'), may hold values from -240 to 240
- page_table: int32 [64, 32], P('req'), may hold values from 0 to 4095, as said below
- cached_len: int32 [64], P('req'), may hold values from 3072 to 4096, as said below
- w_gate_z: bfloat16 [2048, 1536], P(None, 'tp'), may hold values from -0.125 to 0.125
- w_ssm_in: bfloat16 [2048, 1536], P(None, 'tp'), may hold values from -0.125 to 0.125
- w_bc: bfloat16 [2048, 512], replicated, may hold values from -0.125 to 0.125
- w_dt: bfloat16 [2048, 24], P(None, 'tp'), may hold values from -0.125 to 0.125
- conv_w_x: float32 [4, 1536], P(None, 'tp'), may hold values from -3 to 3
- conv_w_bc: float32 [4, 512], replicated, may hold values from -3 to 3
- conv_x_state: bfloat16 [64, 3, 1536], P('req', None, 'tp'), may hold values from -6 to 6
- conv_bc_state: bfloat16 [64, 3, 512], P('req'), may hold values from -6 to 6
- dt_bias: float32 [24], P('tp'), may hold values from -3 to 0
- decay_rate: float32 [24], P('tp'), may hold values from 0.002 to 0.2
- skip_gain: float32 [24], P('tp'), may hold values from 0.5 to 1.5
- mixer_gain: float32 [1536], P('tp'), may hold values from 0.1 to 1.9
- w_mixer_out: bfloat16 [1536, 2048], P('tp'), may hold values from -0.15625 to 0.15625
- ssm_state: float32 [64, 24, 64, 256], P('req', 'tp'), may hold values from -6 to 6
Outputs:
- mixed: bfloat16 [32768, 2048], P('req', 'tp')
- final_state: float32 [64, 24, 64, 256], P('req', 'tp')
Inputs may be any that keep to these rules, and one draw needn't show every extreme that they name: `page_table`: entries are page numbers below 4096. Of one request's 32 entries at most 1 lie among the pages of one index of req, and some request has exactly 1 there. Requests in aligned runs of 4 may share their leading entries. `cached_len`: some request has exactly 4096.
All inputs are finite; a program needn't handle non-finite values.
Results may differ from a plain program's by a relative error of at most 0.018.
The roundings to bfloat16 on the way count: a program that leaves them out, or rounds other values in their place, can miss the bound.
Values may be sent and summed in bfloat16 or wider, within the bound.
A program may use at most 128 MiB of HBM per device.

v0:
```python
from functools import partial

import jax
import jax.numpy as jnp
from jax import lax
from jax.sharding import PartitionSpec as P

HEAD_SIZE = 128
MP = 64
MN = 256
DSSM = 1536


EPSILON = 1e-05
ROPE_BASE = 100000.0
NEG_FILL = -1e30


def rms_scale(value_vectors, gain_row):
    mean_sq = jnp.mean(value_vectors * value_vectors, axis=-1, keepdims=True)
    return value_vectors * lax.rsqrt(mean_sq + EPSILON) * gain_row


def stored(value_vectors):
    return lax.optimization_barrier(value_vectors.astype(jnp.bfloat16))


def apply_rotary(value_vectors, token_positions):
    full_width = value_vectors.shape[-1]
    half_width = full_width // 2
    inverse = ROPE_BASE ** (-2.0 * jnp.arange(half_width, dtype=jnp.float32) / full_width)
    angles = token_positions.astype(jnp.float32)[:, None] * inverse[None, :]
    cosine = jnp.concatenate([jnp.cos(angles), jnp.cos(angles)], axis=-1)[:, None, :]
    sine_row = jnp.concatenate([jnp.sin(angles), jnp.sin(angles)], axis=-1)[:, None, :]
    turned = jnp.concatenate(
        [-value_vectors[..., half_width:], value_vectors[..., :half_width]], axis=-1
    )
    return value_vectors * cosine + turned * sine_row


def short_conv(history, fresh_rows, kernel):
    joined = jnp.concatenate([history, fresh_rows], axis=0).astype(jnp.float32)
    row_count = fresh_rows.shape[0]
    summed = joined[0:row_count] * kernel[0]
    for tap_index in range(1, kernel.shape[0]):
        summed = summed + joined[tap_index : tap_index + row_count] * kernel[tap_index]
    return jax.nn.silu(summed)


def pick_pages(table_row, target, pages_dev, capacity):
    page_count = table_row.shape[0]
    owners = table_row // pages_dev
    local_slot = table_row % pages_dev
    page_index = jnp.arange(page_count, dtype=jnp.int32)
    earlier = (page_index[None, :] < page_index[:, None]) & (owners[None, :] == owners[:, None])
    ranks = jnp.sum(earlier.astype(jnp.int32), axis=1)
    places = jnp.arange(capacity, dtype=jnp.int32)
    chosen = ((owners == target)[:, None] & (ranks[:, None] == places[None, :])).astype(jnp.int32)
    return (
        jnp.sum(chosen * local_slot[:, None], axis=0),
        jnp.sum(chosen * page_index[:, None], axis=0),
        jnp.sum(chosen, axis=0),
    )


def attend(query_rows, key_rows, value_rows, visible, score_scale):
    scores = (
        jnp.einsum("rd,kd->rk", query_rows, key_rows, preferred_element_type=jnp.float32)
        * score_scale
    )
    scores = jnp.where(visible, scores, NEG_FILL)
    row_top = jnp.max(scores, axis=-1, keepdims=True)
    weights = jnp.where(visible, jnp.exp(scores - row_top), 0.0)
    weight_sum = jnp.sum(weights, axis=-1, keepdims=True)
    summed = jnp.dot(weights.astype(jnp.bfloat16), value_rows, preferred_element_type=jnp.float32)
    return (summed, row_top, weight_sum)


def shards(
    tokens,
    attn_gain,
    w_query,
    key_weight,
    value_weight,
    w_attn_out,
    kv_pages,
    page_table,
    cached_len,
    w_gate_z,
    w_ssm_in,
    w_bc,
    w_dt,
    conv_w_x,
    conv_w_bc,
    conv_x_state,
    conv_bc_state,
    dt_bias,
    decay_rate,
    skip_gain,
    mixer_gain,
    w_mixer_out,
    ssm_state,
):
    gathered = lax.all_gather(tokens, "tp", axis=1, tiled=True)
    row_count = gathered.shape[0]
    normed_input = rms_scale(gathered.astype(jnp.float32), attn_gain).astype(jnp.bfloat16)
    length = cached_len[0]
    row_order = jnp.arange(row_count, dtype=jnp.int32)
    token_positions = length + row_order
    query_vectors = apply_rotary(
        jnp.dot(normed_input, w_query, preferred_element_type=jnp.float32).reshape(
            row_count, -1, HEAD_SIZE
        ),
        token_positions,
    ).astype(jnp.bfloat16)
    incoming_keys = apply_rotary(
        jnp.dot(normed_input, key_weight, preferred_element_type=jnp.float32).reshape(
            row_count, -1, HEAD_SIZE
        ),
        token_positions,
    ).astype(jnp.bfloat16)
    incoming_values = (
        jnp.dot(normed_input, value_weight, preferred_element_type=jnp.float32)
        .astype(jnp.bfloat16)
        .reshape(row_count, -1, HEAD_SIZE)
    )
    kv_local = incoming_keys.shape[1]
    devices = lax.axis_size("req")
    pages_dev = kv_pages.shape[0]
    capacity = pages_dev // devices
    page_size = kv_pages.shape[3]
    targets = jnp.arange(devices, dtype=jnp.int32)
    want_slot, page_of, present = jax.vmap(
        partial(pick_pages, page_table[0], pages_dev=pages_dev, capacity=capacity)
    )(targets)
    requested = lax.all_to_all(want_slot, "req", split_axis=0, concat_axis=0, tiled=True)
    fetched = kv_pages[requested.reshape(-1)].reshape((devices, capacity) + kv_pages.shape[1:])
    arrived = lax.all_to_all(fetched, "req", split_axis=0, concat_axis=0, tiled=True)
    cached_key_rows = jnp.transpose(arrived[:, :, 0], (2, 0, 1, 3, 4)).reshape(
        kv_local, -1, HEAD_SIZE
    )
    cached_value_rows = jnp.transpose(arrived[:, :, 1], (2, 0, 1, 3, 4)).reshape(
        kv_local, -1, HEAD_SIZE
    )
    cache_pos = (
        page_of[:, :, None] * page_size + jnp.arange(page_size, dtype=jnp.int32)[None, None, :]
    ).reshape(-1)
    live = jnp.broadcast_to(present[:, :, None] > 0, (devices, capacity, page_size)).reshape(-1) & (
        cache_pos < length
    )
    causal = row_order[None, :] <= row_order[:, None]
    cache_visible = jnp.broadcast_to(live[None, :], (row_count, live.shape[0]))
    score_scale = HEAD_SIZE ** (-0.5)
    head_queries = jnp.transpose(query_vectors, (1, 0, 2))
    key_cache = cached_key_rows[0]
    value_cache = cached_value_rows[0]
    key_fresh = incoming_keys[:, 0]
    value_fresh = incoming_values[:, 0]
    key_all = jnp.concatenate([key_cache, key_fresh], axis=0)
    value_all = jnp.concatenate([value_cache, value_fresh], axis=0)
    visible_all = jnp.concatenate([cache_visible, causal], axis=1)

    def one_head(query_rows):
        head_sum, row_top, head_total = attend(
            query_rows, key_all, value_all, visible_all, score_scale
        )
        return head_sum / head_total

    contexts = [lax.map(one_head, head_queries)]
    context = (
        jnp.transpose(jnp.stack(contexts), (2, 0, 1, 3)).reshape(row_count, -1).astype(jnp.bfloat16)
    )
    attn_part = jnp.dot(context, w_attn_out, preferred_element_type=jnp.float32)
    gate_z = stored(jnp.dot(normed_input, w_gate_z, preferred_element_type=jnp.float32))
    ssm_in = stored(jnp.dot(normed_input, w_ssm_in, preferred_element_type=jnp.float32))
    bc_in = stored(jnp.dot(normed_input, w_bc, preferred_element_type=jnp.float32))
    step_raw = jnp.dot(normed_input, w_dt, preferred_element_type=jnp.float32)
    head_count = w_dt.shape[1]
    ssm_x = stored(short_conv(conv_x_state[0], ssm_in, conv_w_x)).reshape(row_count, head_count, MP)
    bc_rows = stored(short_conv(conv_bc_state[0], bc_in, conv_w_bc))
    b_vectors = bc_rows[:, :MN]
    c_vectors = bc_rows[:, MN:]
    step_size = jax.nn.softplus(step_raw + dt_bias)
    cumulative = jnp.cumsum(-step_size * decay_rate, axis=0)
    gap = cumulative.T[:, :, None] - cumulative.T[:, None, :]
    inner = jnp.dot(c_vectors, b_vectors.T, preferred_element_type=jnp.float32)
    mixing = stored(jnp.where(causal[None], jnp.exp(jnp.minimum(gap, 0.0)), 0.0) * inner[None])
    x_float = ssm_x.astype(jnp.float32)
    moved_float = x_float * step_size[:, :, None]
    moved = stored(moved_float)
    intra = jnp.einsum("hij,jhp->ihp", mixing, moved, preferred_element_type=jnp.float32)
    state_in = ssm_state[0]
    carried = jnp.exp(cumulative)[:, :, None] * jnp.einsum(
        "in,hpn->ihp", c_vectors.astype(jnp.float32), state_in, precision=lax.Precision.HIGHEST
    )
    ssm_y = intra + carried + skip_gain[None, :, None] * x_float
    tail_fade = jnp.exp(cumulative[-1][None, :] - cumulative)
    tail_moved = stored(moved_float * tail_fade[:, :, None])
    last_state = jnp.exp(cumulative[-1])[:, None, None] * state_in + jnp.einsum(
        "jhp,jn->hpn", tail_moved, b_vectors, preferred_element_type=jnp.float32
    )
    gated = ssm_y.reshape(row_count, -1) * jax.nn.silu(gate_z.astype(jnp.float32))
    local_sq = jnp.sum(gated * gated, axis=-1)
    total_sq = lax.psum(local_sq, "tp")
    normed_y = (gated * lax.rsqrt(total_sq / DSSM + EPSILON)[:, None] * mixer_gain).astype(
        jnp.bfloat16
    )
    ssm_part = jnp.dot(normed_y, w_mixer_out, preferred_element_type=jnp.float32)
    summed = lax.psum_scatter(
        (attn_part + ssm_part).astype(jnp.bfloat16), "tp", scatter_dimension=1, tiled=True
    )
    return (summed, last_state[None])


def solution(mesh):
    return jax.shard_map(
        shards,
        mesh=mesh,
        in_specs=(
            P("req", "tp"),
            P(),
            P(None, "tp"),
            P(None, "tp"),
            P(None, "tp"),
            P("tp", None),
            P("req", None, "tp", None, None),
            P("req", None),
            P("req"),
            P(None, "tp"),
            P(None, "tp"),
            P(),
            P(None, "tp"),
            P(None, "tp"),
            P(),
            P("req", None, "tp"),
            P("req", None, None),
            P("tp"),
            P("tp"),
            P("tp"),
            P("tp"),
            P("tp", None),
            P("req", "tp", None, None),
        ),
        out_specs=(P("req", "tp"), P("req", "tp", None, None)),
        check_vma=False,
    )
```

profile of v0, /device:TPU:1, one launch (start us, length us, event | category | flops | bytes accessed | tf_op | source)
XLA Modules:
  0.0 266.5 jit_solution(15106273636629297080)
XLA Ops:
  7.2 0.7 all-gather.2.cloned.1.call-update
  7.9 0.9 and_select_fusion
  8.8 0.7 fusion.61
  9.7 0.7 copy.90
  10.5 12.3 %all-to-all-start = ((s32[64,1,1]{2,1,0:T(1,128)}), s32[64,1,1]{2,1,0:T(1,128)S(1)}, u32[]{:S(2)}, u32[]{:S(2)}) async-start(s32[64,1,1]{2,1,0:T(1,128)} %copy.90), calls=%async_computation | async-start | bytes 65536 | tf_op jit(solution)/shard_map/all_to_all | solution.py:136
  22.9 1.4 fusion.64
  25.0 1.2 multiply_cosine_fusion
  26.3 4.3 %pad_add_fusion = pred[512,8704]{1,0:T(32,128)(4,1)} fusion(pred[512,512]{1,0:T(8,128)(4,1)S(1)} %iota_compare_fusion, pred[8704]{0:T(1024)(128)(4,1)S(1)} %pad.6.clone), kind=kLoop, calls=%fused_computation.17 | loop fusion | flops 4456448 | bytes 4727296 | tf_op jit(solution)/shard_map/concatenate | solution.py:161
  30.7 1.3 all-to-all-done
  32.0 1.2 reduce.3
  33.2 5.3 %gather_fusion = bf16[64,2,128,128]{3,2,1,0:T(8,128)(2,1)} fusion(bf16[64,2,128,128]{3,2,1,0:T(8,128)(2,1)} %bitcast.142, s32[1024]{0:T(1024)S(1)} %pad_clamp_fusion), kind=kCustom, calls=%fused_computation | custom fusion | bytes 8388864 | tf_op jit(solution)/shard_map/gather | solution.py:137
  38.5 9.3 %all-to-all-start.1 = ((bf16[64,1,2,1,128,128]{5,4,2,3,1,0:T(8,128)(2,1)}), bf16[64,1,2,1,128,128]{5,4,2,3,1,0:T(8,128)(2,1)}, u32[]{:S(2)}, u32[]{:S(2)}) async-start(bf16[64,1,2,1,128,128]{5,4,2,3,1,0:T(8,128)(2,1)} %bitcast.136), calls=%async_computation.1 | async-start | bytes 8388608 | tf_op jit(solution)/shard_map/all_to_all | solution.py:138
  47.8 0.5 reduce-scatter.2.cloned.1.call-start
  48.7 2.2 fusion.18
  51.0 0.5 fusion.20
  51.6 1.3 copy-done.2
  52.9 0.7 fusion.51
  53.6 1.2 reduce-window.6
  55.3 4.3 %convolution_convert_fusion.1 = bf16[512,768]{1,0:T(8,128)(2,1)S(1)} fusion(bf16[512,2048]{1,0:T(8,128)(2,1)} %copy-done.2, bf16[2048,768]{1,0:T(8,128)(2,1)} %param.35), kind=kOutput, calls=%fused_computation.48 | convolution fusion | flops 1611005952 | bytes 6029312 | tf_op jit(solution)/shard_map/dot_general | solution.py:175
  59.8 1.8 multiply_convert_fusion.3
  61.7 2.6 copy.93
  64.3 2.7 %multiply_convert_fusion.1 = (bf16[512,12,64]{0,2,1:T(8,128)(2,1)}, bf16[512,12,64]{0,2,1:T(8,128)(2,1)S(1)}) fusion(f32[512,12,64]{0,2,1:T(8,128)} %bitcast.137, f32[512,12]{0,1:T(8,128)S(1)} %get-tuple-element.67, f32[512,12]{0,1:T(8,128)S(1)} %get-tuple-element.79), kind=kLoop, calls=%fused_computation.42 | loop fusion | flops 1572864 | bytes 3194880 | tf_op jit(solution)/shard_map/convert_element_type | solution.py:25
  67.1 2.9 %convolution_convert_fusion.2 = bf16[512,512]{1,0:T(8,128)(2,1)S(1)} fusion(bf16[512,2048]{1,0:T(8,128)(2,1)S(1)} %copy-done.3, bf16[2048,512]{1,0:T(8,128)(2,1)} %param.36), kind=kOutput, calls=%fused_computation.49 | convolution fusion | flops 1074003968 | bytes 4718592 | tf_op jit(solution)/shard_map/dot_general | solution.py:176
  70.1 0.6 multiply_convert_fusion.5
  71.1 3.3 %multiply_convert_fusion = bf16[12,512,512]{2,1,0:T(8,128)(2,1)S(1)} fusion(f32[512,512]{1,0:T(8,128)S(1)} %fusion.45, f32[12,512]{1,0:T(8,128)S(1)} %bitcast.148, pred[512,512]{1,0:T(8,128)(4,1)S(1)} %iota_compare_fusion), kind=kLoop, calls=%fused_computation.18 | loop fusion | flops 15728640 | bytes 7626752 | tf_op jit(solution)/shard_map/convert_element_type | solution.py:25
  74.4 2.0 fusion.67
  76.4 2.2 fusion.28
  78.7 3.0 %copy.96 = f32[512,768]{1,0:T(8,128)} copy(f32[512,768]{0,1:T(8,128)} %bitcast.141) | data formatting | bytes 3145728 | tf_op jit(solution)/shard_map/reshape | solution.py:202
  81.7 5.3 %convolution_convert_fusion = bf16[512,768]{1,0:T(8,128)(2,1)} fusion(bf16[512,2048]{1,0:T(8,128)(2,1)} %copy-done.2, bf16[2048,768]{1,0:T(8,128)(2,1)} %param.34), kind=kOutput, calls=%fused_computation.47 | convolution fusion | flops 1611005952 | bytes 6029312 | tf_op jit(solution)/shard_map/dot_general | solution.py:174
  87.1 0.8 fusion.66
  88.0 0.8 fusion.41
  88.9 1.1 copy.85
  89.9 1.8 copy.89
  91.7 4.5 %fusion.65 = f32[512,512]{0,1:T(8,128)} fusion(bf16[512,2048]{1,0:T(8,128)(2,1)} %copy-done.2, bf16[2048,512]{1,0:T(8,128)(2,1)} %param.27), kind=kOutput, calls=%fused_computation.145 | convolution fusion | flops 1073741824 | bytes 5242880 | tf_op jit(solution)/shard_map/dot_general | solution.py:111
  96.2 2.5 copy.86
  98.7 1.0 copy.91
  99.8 2.2 multiply_reduce_fusion
  102.0 3.8 %psum.7 = f32[512]{0:T(512)S(1)} all-reduce(f32[512]{0:T(512)S(1)} %multiply_reduce_fusion), channel_id=1, replica_groups=mesh['req'=64,'tp'=2] {'tp'}, use_global_device_ids=true, to_apply=%region_12.13 | all-reduce | flops 512 | bytes 4096 | tf_op jit(solution)/shard_map/psum | solution.py:204
  105.7 2.0 slice_negate_fusion
  107.8 1.1 fusion.39
  108.9 0.6 copy-done.5
  109.7 0.7 convolution_convert_fusion.3
  110.4 0.7 copy-done.9
  111.3 4.1 %fusion.35 = f32[512,2048]{1,0:T(8,128)} fusion(bf16[768,2048]{1,0:T(8,128)(2,1)S(1)} %copy-done, f32[768]{0:T(1024)S(1)} %copy-done.31, f32[512]{0:T(512)S(1)} %add_rsqrt_fusion, f32[512,768]{1,0:T(8,128)S(1)} %copy-done.9, bf16[512,768]{1,0:T(8,128)(2,1)S(1)} %copy-done.14), kind=kOutput, calls=%fused_computation.68 | convolution fusion | flops 1614151680 | bytes 9704448 | tf_op jit(solution)/shard_map/dot_general | solution.py:208
  115.4 2.7 %fusion.63 = (bf16[64,1,1,1,128,128]{5,4,2,3,1,0:T(8,128)(2,1)S(1)}, bf16[64,1,1,1,128,128]{5,4,2,3,1,0:T(8,128)(2,1)S(1)}) fusion(bf16[64,1,2,1,128,128]{5,4,2,3,1,0:T(8,128)(2,1)} %all-to-all-done.1), kind=kLoop, calls=%fused_computation.143 | loop fusion | bytes 8388608 | tf_op jit(solution)/shard_map/slice | solution.py:142
  118.1 4.7 %pad_maximum_fusion = bf16[8704,128]{1,0:T(8,128)(2,1)S(1)} fusion(bf16[512,128]{1,0:T(8,128)(2,1)S(1)} %copy.91, bf16[8192,128]{1,0:T(8,128)(2,1)S(1)} %bitcast.140), kind=kLoop, calls=%fused_computation.25 | loop fusion | flops 4456448 | bytes 4456448 | tf_op jit(solution)/shard_map/concatenate | solution.py:159
  122.9 5.5 %pad_maximum_fusion.1 = bf16[8704,128]{1,0:T(8,128)(2,1)} fusion(bf16[512,128]{1,0:T(8,128)(2,1)S(1)} %convolution_convert_fusion.3, bf16[8192,128]{1,0:T(8,128)(2,1)S(1)} %bitcast.139), kind=kLoop, calls=%fused_computation.26 | loop fusion | flops 4456448 | bytes 4456448 | tf_op jit(solution)/shard_map/concatenate | solution.py:160
  128.4 89.0 %while.10 = (s32[]{:T(128)}, bf16[4,512,128]{1,2,0:T(8,128)(2,1)S(1)}, bf16[4,512,128]{2,1,0:T(8,128)(2,1)}, bf16[8704,128]{1,0:T(8,128)(2,1)S(1)}, pred[512,870...) while((s32[]{:T(128)}, bf16[4,512,128]{1,2,0:T(8,128)(2,1)S(1)}, bf16[4,512,128]{2,1,0:T(8,128)(2,1)}, ...), condition=%wide.region_8.9_spmd, body=%wide.region_5.8_spmd.sunk | while | flops 2339765248 | bytes 85469824 | solution.py:169
  128.4 6.0 %fusion.99 = (f32[512]{0:T(512)S(1)}, f32[512,8704]{1,0:T(8,128)S(1)}) fusion(pred[512,8704]{1,0:T(32,128)(4,1)} %get-tuple-element.139, bf16[8704,128]{1,0:T(8,128)(2,1)S(1)} %get-tuple-element.138, bf16[4,512,128]{2,1,0:T(8,128)(2,1)} %get-tuple-element.137, s32[]{:T(128)} %get-tuple-element.128), kind=kOutput, calls=%fused_computation.3.clone.1 | convolution fusion | flops 1154219520 | bytes 24644096 | tf_op jit(solution)/shard_map/while/body/eval_jaxpr/rd,kd->rk/dot_general | solution.py:68
  134.4 5.8 %fusion.100 = f32[512]{0:T(512)S(1)} fusion(pred[512,8704]{1,0:T(32,128)(4,1)S(1)} %bitcast.135, f32[512,8704]{1,0:T(8,128)S(1)} %get-tuple-element.119, f32[512]{0:T(512)S(1)} %get-tuple-element.120), kind=kLoop, calls=%fused_computation.4.clone.1 | loop fusion | flops 22281728 | bytes 22286336 | tf_op jit(solution)/shard_map/while/body/eval_jaxpr/reduce_sum | solution.py:74
  140.2 10.3 %fusion.101 = bf16[1,512,128]{2,1,0:T(8,128)(2,1)S(1)} fusion(bf16[8704,128]{1,0:T(8,128)(2,1)} %get-tuple-element.140, pred[512,8704]{1,0:T(32,128)(4,1)} %get-tuple-element.139, f32[512,8704]{1,0:T(8,128)S(1)} %get-tuple-element.119, f32[512]{0:T(512)S(1)} %get-tuple-element.120, f32[512]{0:T(512)S(1)} %fusion.100), kind=kOutput, calls=%fused_computation.8.clone.1 | convolution fusion | flops 1163264000 | bytes 24645632 | tf_op jit(solution)/shard_map/while/body/eval_jaxpr/dot_general | solution.py:75
  150.6 6.0 %fusion.99 = (f32[512]{0:T(512)S(1)}, f32[512,8704]{1,0:T(8,128)S(1)}) fusion(pred[512,8704]{1,0:T(32,128)(4,1)} %get-tuple-element.139, bf16[8704,128]{1,0:T(8,128)(2,1)S(1)} %get-tuple-element.138, bf16[4,512,128]{2,1,0:T(8,128)(2,1)} %get-tuple-element.137, s32[]{:T(128)} %get-tuple-element.128), kind=kOutput, calls=%fused_computation.3.clone.1 | convolution fusion | flops 1154219520 | bytes 24644096 | tf_op jit(solution)/shard_map/while/body/eval_jaxpr/rd,kd->rk/dot_general | solution.py:68
  156.7 5.8 %fusion.100 = f32[512]{0:T(512)S(1)} fusion(pred[512,8704]{1,0:T(32,128)(4,1)S(1)} %bitcast.135, f32[512,8704]{1,0:T(8,128)S(1)} %get-tuple-element.119, f32[512]{0:T(512)S(1)} %get-tuple-element.120), kind=kLoop, calls=%fused_computation.4.clone.1 | loop fusion | flops 22281728 | bytes 22286336 | tf_op jit(solution)/shard_map/while/body/eval_jaxpr/reduce_sum | solution.py:74
  162.4 10.3 %fusion.101 = bf16[1,512,128]{2,1,0:T(8,128)(2,1)S(1)} fusion(bf16[8704,128]{1,0:T(8,128)(2,1)} %get-tuple-element.140, pred[512,8704]{1,0:T(32,128)(4,1)} %get-tuple-element.139, f32[512,8704]{1,0:T(8,128)S(1)} %get-tuple-element.119, f32[512]{0:T(512)S(1)} %get-tuple-element.120, f32[512]{0:T(512)S(1)} %fusion.100), kind=kOutput, calls=%fused_computation.8.clone.1 | convolution fusion | flops 1163264000 | bytes 24645632 | tf_op jit(solution)/shard_map/while/body/eval_jaxpr/dot_general | solution.py:75
  172.9 6.0 %fusion.99 = (f32[512]{0:T(512)S(1)}, f32[512,8704]{1,0:T(8,128)S(1)}) fusion(pred[512,8704]{1,0:T(32,128)(4,1)} %get-tuple-element.139, bf16[8704,128]{1,0:T(8,128)(2,1)S(1)} %get-tuple-element.138, bf16[4,512,128]{2,1,0:T(8,128)(2,1)} %get-tuple-element.137, s32[]{:T(128)} %get-tuple-element.128), kind=kOutput, calls=%fused_computation.3.clone.1 | convolution fusion | flops 1154219520 | bytes 24644096 | tf_op jit(solution)/shard_map/while/body/eval_jaxpr/rd,kd->rk/dot_general | solution.py:68
  178.9 5.8 %fusion.100 = f32[512]{0:T(512)S(1)} fusion(pred[512,8704]{1,0:T(32,128)(4,1)S(1)} %bitcast.135, f32[512,8704]{1,0:T(8,128)S(1)} %get-tuple-element.119, f32[512]{0:T(512)S(1)} %get-tuple-element.120), kind=kLoop, calls=%fused_computation.4.clone.1 | loop fusion | flops 22281728 | bytes 22286336 | tf_op jit(solution)/shard_map/while/body/eval_jaxpr/reduce_sum | solution.py:74
  184.7 10.3 %fusion.101 = bf16[1,512,128]{2,1,0:T(8,128)(2,1)S(1)} fusion(bf16[8704,128]{1,0:T(8,128)(2,1)} %get-tuple-element.140, pred[512,8704]{1,0:T(32,128)(4,1)} %get-tuple-element.139, f32[512,8704]{1,0:T(8,128)S(1)} %get-tuple-element.119, f32[512]{0:T(512)S(1)} %get-tuple-element.120, f32[512]{0:T(512)S(1)} %fusion.100), kind=kOutput, calls=%fused_computation.8.clone.1 | convolution fusion | flops 1163264000 | bytes 24645632 | tf_op jit(solution)/shard_map/while/body/eval_jaxpr/dot_general | solution.py:75
  195.1 6.0 %fusion.99 = (f32[512]{0:T(512)S(1)}, f32[512,8704]{1,0:T(8,128)S(1)}) fusion(pred[512,8704]{1,0:T(32,128)(4,1)} %get-tuple-element.139, bf16[8704,128]{1,0:T(8,128)(2,1)S(1)} %get-tuple-element.138, bf16[4,512,128]{2,1,0:T(8,128)(2,1)} %get-tuple-element.137, s32[]{:T(128)} %get-tuple-element.128), kind=kOutput, calls=%fused_computation.3.clone.1 | convolution fusion | flops 1154219520 | bytes 24644096 | tf_op jit(solution)/shard_map/while/body/eval_jaxpr/rd,kd->rk/dot_general | solution.py:68
  201.1 5.8 %fusion.100 = f32[512]{0:T(512)S(1)} fusion(pred[512,8704]{1,0:T(32,128)(4,1)S(1)} %bitcast.135, f32[512,8704]{1,0:T(8,128)S(1)} %get-tuple-element.119, f32[512]{0:T(512)S(1)} %get-tuple-element.120), kind=kLoop, calls=%fused_computation.4.clone.1 | loop fusion | flops 22281728 | bytes 22286336 | tf_op jit(solution)/shard_map/while/body/eval_jaxpr/reduce_sum | solution.py:74
  206.9 10.3 %fusion.101 = bf16[1,512,128]{2,1,0:T(8,128)(2,1)S(1)} fusion(bf16[8704,128]{1,0:T(8,128)(2,1)} %get-tuple-element.140, pred[512,8704]{1,0:T(32,128)(4,1)} %get-tuple-element.139, f32[512,8704]{1,0:T(8,128)S(1)} %get-tuple-element.119, f32[512]{0:T(512)S(1)} %get-tuple-element.120, f32[512]{0:T(512)S(1)} %fusion.100), kind=kOutput, calls=%fused_computation.8.clone.1 | convolution fusion | flops 1163264000 | bytes 24645632 | tf_op jit(solution)/shard_map/while/body/eval_jaxpr/dot_general | solution.py:75
  217.3 5.4 %add_convert_fusion = bf16[512,2048]{1,0:T(8,128)(2,1)} fusion(f32[512,2048]{1,0:T(8,128)} %fusion.35, bf16[512,512]{0,1:T(8,128)(2,1)S(1)} %bitcast.144, bf16[512,2048]{1,0:T(8,128)(2,1)} %param.30), kind=kOutput, calls=%fused_computation.24 | convolution fusion | flops 1075838976 | bytes 8912896 | tf_op jit(solution)/shard_map/dot_general | solution.py:173
  222.8 0.6 copy-done.27
  223.4 3.0 %fusion.29 = f32[1,12,64,256]{3,2,1,0:T(8,128)} fusion(bf16[512,12,64]{0,2,1:T(8,128)(2,1)} %get-tuple-element.58, f32[1,12,64,256]{3,2,1,0:T(8,128)} %param.47, f32[12]{0:T(128)S(1)} %exp.44, bf16[512,512]{1,0:T(8,128)(2,1)} %copy-done.10), kind=kOutput, calls=%fused_computation.51 | convolution fusion | flops 201719808 | bytes 2621488 | tf_op jit(solution)/shard_map/jhp,jn->hpn/dot_general | solution.py:199
  226.4 33.0 %reduce-scatter.2.cloned.1.call-done = bf16[512,1024]{1,0:T(8,128)(2,1)} async-done(((bf16[512,2048]{1,0:T(8,128)(2,1)}), bf16[512,1024]{1,0:T(8,128)(2,1)}) %reduce-scatter.2.cloned.1.call-update) | async-done | bytes 1048592 | tf_op jit(solution)/shard_map/reduce_scatter | solution.py:209
  (124 shorter events, 3.3 us)
Async XLA Ops:
  7.2 103.2 %copy-start = (bf16[768,2048]{1,0:T(8,128)(2,1)S(1)}, bf16[768,2048]{1,0:T(8,128)(2,1)}, u32[]{:S(2)}) copy-start(bf16[768,2048]{1,0:T(8,128)(2,1)} %param.46) | copy-start | bytes 9437188
  7.2 41.5 %all-gather.2.cloned.1.call-start = ((), (), s32[]{:S(2)}) async-start(), calls=%async_computation.3 | async-start | bytes 3145728 | tf_op jit(solution)/shard_map/all_gather | solution.py:104
  10.5 21.5 %all-to-all-start = ((s32[64,1,1]{2,1,0:T(1,128)}), s32[64,1,1]{2,1,0:T(1,128)S(1)}, u32[]{:S(2)}, u32[]{:S(2)}) async-start(s32[64,1,1]{2,1,0:T(1,128)} %copy.90), calls=%async_computation | async-start | bytes 65536 | tf_op jit(solution)/shard_map/all_to_all | solution.py:136
  26.3 4.3 %copy-start.20 = (f32[4,768]{1,0:T(4,128)S(1)}, f32[4,768]{1,0:T(4,128)}, u32[]{:S(2)}) copy-start(f32[4,768]{1,0:T(4,128)} %param.38) | copy-start | bytes 36868
  38.5 12.5 %copy-start.21 = (f32[2048]{0:T(1024)S(1)}, f32[2048]{0:T(1024)}, u32[]{:S(2)}) copy-start(f32[2048]{0:T(1024)} %param.26) | copy-start | bytes 24580
  38.5 76.9 %all-to-all-start.1 = ((bf16[64,1,2,1,128,128]{5,4,2,3,1,0:T(8,128)(2,1)}), bf16[64,1,2,1,128,128]{5,4,2,3,1,0:T(8,128)(2,1)}, u32[]{:S(2)}, u32[]{:S(2)}) async-start(bf16[64,1,2,1,128,128]{5,4,2,3,1,0:T(8,128)(2,1)} %bitcast.136), calls=%async_computation.1 | async-start | bytes 8388608 | tf_op jit(solution)/shard_map/all_to_all | solution.py:138
  47.8 211.6 %reduce-scatter.2.cloned.1.call-start = ((), (), s32[]{:S(2)}) async-start(), calls=%async_computation.4 | async-start | bytes 3145728 | tf_op jit(solution)/shard_map/reduce_scatter | solution.py:209
  48.7 2.2 copy-start.8
  51.0 1.9 copy-start.19
  51.0 1.9 copy-start.29
  51.0 1.9 copy-start.30
  51.6 1.4 copy-start.2
  55.3 8.9 %copy-start.26 = (f32[12]{0:T(128)}, f32[12]{0:T(128)S(1)}, u32[]{:S(2)}) copy-start(f32[12]{0:T(128)S(1)} %slice_reduce_fusion.1) | copy-start | bytes 148
  55.3 4.3 %copy-start.24 = (bf16[1,3,768]{2,1,0:T(4,128)(2,1)S(1)}, bf16[1,3,768]{2,1,0:T(4,128)(2,1)}, u32[]{:S(2)}) copy-start(bf16[1,3,768]{2,1,0:T(4,128)(2,1)} %param.40) | copy-start | bytes 13828
  64.2 2.8 %copy-start.3 = (bf16[512,2048]{1,0:T(8,128)(2,1)S(1)}, bf16[512,2048]{1,0:T(8,128)(2,1)}, u32[]{:S(2)}) copy-start(bf16[512,2048]{1,0:T(8,128)(2,1)} %copy-done.2) | copy-start | bytes 6291460
  67.1 2.9 %copy-start.25 = (bf16[1,3,512]{2,1,0:T(4,128)(2,1)S(1)}, bf16[1,3,512]{2,1,0:T(4,128)(2,1)}, u32[]{:S(2)}) copy-start(bf16[1,3,512]{2,1,0:T(4,128)(2,1)} %param.41) | copy-start | bytes 9220
  67.1 3.0 %copy-start.22 = (f32[1,512]{1,0:T(1,128)S(1)}, f32[1,512]{1,0:T(1,128)}, u32[]{:S(2)}) copy-start(f32[1,512]{1,0:T(1,128)} %get-tuple-element.71) | copy-start | bytes 6148
  67.1 3.1 %copy-start.23 = (f32[1,512]{1,0:T(1,128)S(1)}, f32[1,512]{1,0:T(1,128)}, u32[]{:S(2)}) copy-start(f32[1,512]{1,0:T(1,128)} %get-tuple-element.72) | copy-start | bytes 6148
  70.8 5.6 %copy-start.10 = (bf16[512,512]{1,0:T(8,128)(2,1)}, bf16[512,512]{1,0:T(8,128)(2,1)S(1)}, u32[]{:S(2)}) copy-start(bf16[512,512]{1,0:T(8,128)(2,1)S(1)} %multiply_convert_fusion.5) | copy-start | bytes 1572868
  74.4 2.0 copy-start.7
  74.4 2.0 copy-start.11
  74.4 2.0 copy-start.28
  81.7 5.3 %copy-start.4 = (bf16[512,2048]{1,0:T(8,128)(2,1)S(1)}, bf16[512,2048]{1,0:T(8,128)(2,1)}, u32[]{:S(2)}) copy-start(bf16[512,2048]{1,0:T(8,128)(2,1)} %copy-done.2) | copy-start | bytes 6291460
  81.7 5.3 %copy-start.15 = (bf16[2048,128]{1,0:T(8,128)(2,1)S(1)}, bf16[2048,128]{1,0:T(8,128)(2,1)}, u32[]{:S(2)}) copy-start(bf16[2048,128]{1,0:T(8,128)(2,1)} %param.28) | copy-start | bytes 1572868
  87.0 0.9 copy-start.17
  87.0 1.0 copy-start.18
  105.7 2.0 copy-start.6
  105.7 2.0 copy-start.13
  107.8 1.8 copy-start.5
  107.8 1.9 copy-start.16
  109.6 1.4 copy-start.9
  109.6 1.6 copy-start.14
  109.7 1.6 copy-start.31
  122.8 5.5 %copy-start.12 = (bf16[4,512,128]{1,2,0:T(8,128)(2,1)S(1)}, bf16[4,512,128]{1,2,0:T(8,128)(2,1)}, u32[]{:S(2)}) copy-start(bf16[4,512,128]{1,2,0:T(8,128)(2,1)} %custom-call.2) | copy-start | bytes 1572868
  128.4 6.0 %slice-start = ((s8[4456448]{0:T(1024)(128)(4,1)}), s8[4194304]{0:T(1024)(128)(4,1)S(1)}, s32[]{:S(2)}) async-start(s8[4456448]{0:T(1024)(128)(4,1)} %bitcast.134), calls=%async_computation.5 | async-start | bytes 8388608 | tf_op jit(solution)/shard_map/while
  128.4 6.0 %slice-start.1 = ((s8[4456448]{0:T(1024)(128)(4,1)}), s8[262144]{0:T(1024)(128)(4,1)S(1)}, s32[]{:S(2)}) async-start(s8[4456448]{0:T(1024)(128)(4,1)} %bitcast.134), calls=%async_computation.6 | async-start | bytes 524288 | tf_op jit(solution)/shard_map/while
  150.6 6.0 %slice-start = ((s8[4456448]{0:T(1024)(128)(4,1)}), s8[4194304]{0:T(1024)(128)(4,1)S(1)}, s32[]{:S(2)}) async-start(s8[4456448]{0:T(1024)(128)(4,1)} %bitcast.134), calls=%async_computation.5 | async-start | bytes 8388608 | tf_op jit(solution)/shard_map/while
  150.6 6.0 %slice-start.1 = ((s8[4456448]{0:T(1024)(128)(4,1)}), s8[262144]{0:T(1024)(128)(4,1)S(1)}, s32[]{:S(2)}) async-start(s8[4456448]{0:T(1024)(128)(4,1)} %bitcast.134), calls=%async_computation.6 | async-start | bytes 524288 | tf_op jit(solution)/shard_map/while
  172.8 6.0 %slice-start = ((s8[4456448]{0:T(1024)(128)(4,1)}), s8[4194304]{0:T(1024)(128)(4,1)S(1)}, s32[]{:S(2)}) async-start(s8[4456448]{0:T(1024)(128)(4,1)} %bitcast.134), calls=%async_computation.5 | async-start | bytes 8388608 | tf_op jit(solution)/shard_map/while
  172.9 6.0 %slice-start.1 = ((s8[4456448]{0:T(1024)(128)(4,1)}), s8[262144]{0:T(1024)(128)(4,1)S(1)}, s32[]{:S(2)}) async-start(s8[4456448]{0:T(1024)(128)(4,1)} %bitcast.134), calls=%async_computation.6 | async-start | bytes 524288 | tf_op jit(solution)/shard_map/while
  195.1 6.0 %slice-start = ((s8[4456448]{0:T(1024)(128)(4,1)}), s8[4194304]{0:T(1024)(128)(4,1)S(1)}, s32[]{:S(2)}) async-start(s8[4456448]{0:T(1024)(128)(4,1)} %bitcast.134), calls=%async_computation.5 | async-start | bytes 8388608 | tf_op jit(solution)/shard_map/while
  195.1 6.0 %slice-start.1 = ((s8[4456448]{0:T(1024)(128)(4,1)}), s8[262144]{0:T(1024)(128)(4,1)S(1)}, s32[]{:S(2)}) async-start(s8[4456448]{0:T(1024)(128)(4,1)} %bitcast.134), calls=%async_computation.6 | async-start | bytes 524288 | tf_op jit(solution)/shard_map/while
  222.8 0.6 copy-start.27
  222.8 36.7 %copy-start.1 = (bf16[768,2048]{1,0:T(8,128)(2,1)S(1)}, bf16[768,2048]{1,0:T(8,128)(2,1)}, u32[]{:S(2)}) copy-start(bf16[768,2048]{1,0:T(8,128)(2,1)} %param.46) | copy-start | bytes 9437188
Sparse Core Ops, SparseCore 0:
  9.6 39.0 all-gather.1
  222.9 36.4 reduce-scatter.1
where the time goes:
time: 271 us; the launch traced here: 267 us
  matrix products  101 us (37%)
  other arithmetic  61.1 us (23%)
  waiting for transfers between devices  35.4 us (13%)
  local copies, waits for them, and re-layouts  26.9 us (10%)
  starting transfers between devices  22.2 us (8%)
  between operations  15.4 us (6%)
  blocking collectives  3.78 us (1%)
    dot_general x4, matrix products, attend(): jnp.dot(weights.astype(jnp.bfloat16), value_rows, preferred_element_type=...  41.1 us
    reduce_scatter x1, waiting for transfers between devices, shards(): lax.psum_scatter((attn_part + ssm_part).astype(jnp.bfloat16), 'tp', scatt...  33 us
    dot_general x4, matrix products, attend(): jnp.einsum('rd,kd->rk', query_rows, key_rows, preferred_element_type=jnp....  24 us
    reduce_sum x4, other arithmetic, attend(): weight_sum = jnp.sum(weights, axis=-1, keepdims=True)  23 us
    all_to_all x1, starting transfers between devices, shards(): lax.all_to_all(want_slot, 'req', split_axis=0, concat_axis=0, tiled=True)  12.3 us
    all_to_all x1, starting transfers between devices, shards(): lax.all_to_all(fetched, 'req', split_axis=0, concat_axis=0, tiled=True)  9.35 us
    convert_element_type x4, other arithmetic, stored(): return lax.optimization_barrier(value_vectors.astype(jnp.bfloat16))  8.46 us
    concatenate x1, other arithmetic, shards(): value_all = jnp.concatenate([value_cache, value_fresh], axis=0)  5.52 us
  transfers between devices with their start and end apart: 4, of which 3 were waited for; matrix products, arithmetic and copies ran while one was open for 29% of the time, Pallas kernels for 0%

commit v1 on v0

v1 whole, which is shorter than its diff:
```python
import math
from functools import partial

import jax
import jax.numpy as jnp
from jax import lax
from jax.experimental import pallas as pl
from jax.experimental.pallas import tpu as pltpu
from jax.sharding import PartitionSpec as P

HEAD = 128
MP = 64
MN = 256
DSSM = 1536
EPSILON = 1e-05
ROPE_BASE = 100000.0
NEG_FILL = -1e30
T = 512
CH = 128
F32 = jnp.float32
BF16 = jnp.bfloat16
MESH = pl.DeviceIdType.MESH


def dot(a, b):
    return lax.dot_general(a, b, (((1,), (0,)), ((), ())), preferred_element_type=F32)


def dot_nt(a, b):
    return lax.dot_general(a, b, (((1,), (1,)), ((), ())), preferred_element_type=F32)


def dot_tn(a, b):
    return lax.dot_general(a, b, (((0,), (0,)), ((), ())), preferred_element_type=F32)


def sigmoid(v):
    return 1.0 / (1.0 + jnp.exp(-v))


def split3(v):
    hi = v.astype(BF16)
    rest = v - hi.astype(F32)
    mid = rest.astype(BF16)
    low = (rest - mid.astype(F32)).astype(BF16)
    return hi, mid, low


def project_kernel(
    tok, gain, cos, sin, wdt, bias, decay, convw, hist, skip, state,
    wq, wk, wv, wx, wbc, wz,
    q_out, k_out, v_out, gated, sq_out, final,
    w, normed, proj, ub, xbc, inner, cs, cumt, cumcol, stepcol, sqs, sems,
):
    hq, hx, hn = wq.shape[1], wx.shape[1], wbc.shape[1]
    offs = [0, hq, hq + HEAD]
    base = hq + 2 * HEAD
    offs += [base, base + hx, base + hx + hn]
    copies = []
    for i, (src, off) in enumerate(zip((wq, wk, wv, wx, wbc, wz), offs)):
        cp = pltpu.make_async_copy(src, w.at[:, pl.ds(off, src.shape[1])], sems.at[i])
        cp.start()
        copies.append(cp)

    def norm_rows(i, carry):
        rows = pl.ds(pl.multiple_of(i * 64, 64), 64)
        v = tok[rows, :].astype(F32)
        mean_sq = jnp.mean(v * v, axis=-1, keepdims=True)
        normed[rows, :] = (v * lax.rsqrt(mean_sq + EPSILON) * gain[...]).astype(BF16)
        return carry

    lax.fori_loop(0, T // 64, norm_rows, 0)

    step_raw = dot(normed[...], wdt[...])
    v = step_raw + bias[...]
    step = jnp.maximum(v, 0.0) + jnp.log1p(jnp.exp(-jnp.abs(v)))
    ri = lax.broadcasted_iota(jnp.int32, (T, T), 0)
    ci = lax.broadcasted_iota(jnp.int32, (T, T), 1)
    tri = jnp.where(ri >= ci, 1.0, 0.0).astype(BF16)
    hi, mid, low = split3(-step * decay[...])
    cum = dot(tri, hi) + (dot(tri, mid) + dot(tri, low))
    cumt[...] = cum.T
    heads = skip.shape[0]
    for h in range(heads):
        cumcol[h] = jnp.broadcast_to(cum[:, h : h + 1], (T, 128))
        stepcol[h] = jnp.broadcast_to(step[:, h : h + 1], (T, 128))

    def rope(u):
        return (u * cos[...] + pltpu.roll(u, HEAD // 2, 1) * sin[...]).astype(BF16)

    for i in range(3):
        copies[i].wait()
    for n in range(hq // 256):
        acc = dot(normed[...], w[:, n * 256 : (n + 1) * 256])
        for k in range(2):
            u = rope(acc[:, k * 128 : (k + 1) * 128])
            h = n * 2 + k
            for c in range(T // CH):
                q_out[c, h * CH : (h + 1) * CH, :] = u[c * CH : (c + 1) * CH]
    acc = dot(normed[...], w[:, hq : hq + 256])
    k_out[...] = rope(acc[:, :128])
    v_out[...] = acc[:, 128:].astype(BF16)

    def proj_tile(n, carry):
        o = pl.multiple_of(n * 256, 256)
        proj[:, pl.ds(o, 256)] = dot(normed[...], w[:, pl.ds(base + o, 256)]).astype(BF16)
        return carry

    copies[3].wait()
    copies[4].wait()
    nconv = (hx + hn) // 256
    lax.fori_loop(0, nconv, proj_tile, 0)

    def conv_tile(n, carry):
        cols = pl.ds(pl.multiple_of(n * 128, 128), 128)
        ub[0:8, :] = hist[:, cols]
        ub[8 : T + 8, :] = proj[:, cols].astype(F32)
        taps = convw[:, cols]
        s = ub[5 : T + 5, :] * taps[0:1]
        s = s + ub[6 : T + 6, :] * taps[1:2]
        s = s + ub[7 : T + 7, :] * taps[2:3]
        s = s + ub[8 : T + 8, :] * taps[3:4]
        xbc[:, cols] = (s * sigmoid(s)).astype(BF16)
        return carry

    lax.fori_loop(0, (hx + hn) // 128, conv_tile, 0)
    copies[5].wait()
    lax.fori_loop(nconv, nconv + hx // 256, proj_tile, 0)

    bv = xbc[:, hx : hx + MN]
    cv = xbc[:, hx + MN :]
    inner[...] = dot_nt(cv, bv)
    st = state[...].reshape(hx, MN)
    st_hi = st.astype(BF16)
    st_lo = (st - st_hi.astype(F32)).astype(BF16)
    cs[...] = dot_nt(cv, st_hi) + dot_nt(cv, st_lo)
    sqs[...] = jnp.zeros_like(sqs)
    left = lax.broadcasted_iota(jnp.int32, (T, 128), 1) < MP
    left_row = lax.broadcasted_iota(jnp.int32, (1, 128), 1) < MP
    half = T // 2
    rb_i = lax.broadcasted_iota(jnp.int32, (half, half), 0)
    rb_j = lax.broadcasted_iota(jnp.int32, (half, half), 1)
    causal = rb_j <= rb_i

    def pair(p, carry):
        cols = pl.ds(pl.multiple_of(p * 128, 128), 128)
        ha = 2 * p
        hb = ha + 1
        xp = xbc[:, cols].astype(F32)
        stp = jnp.where(left, stepcol[ha], stepcol[hb])
        cup = jnp.where(left, cumcol[ha], cumcol[hb])
        moved_f = xp * stp
        moved = moved_f.astype(BF16)
        zero = jnp.zeros_like(moved)
        ma = jnp.where(left, moved, zero)
        mb = jnp.where(left, zero, moved)
        parts = []
        for rb in range(2):
            rows = slice(rb * half, (rb + 1) * half)
            total = None
            for h, mv in ((ha, ma), (hb, mb)):
                col = cumcol[h, rows, :]
                col = jnp.concatenate([col, col], axis=1)
                for jb in range(rb + 1):
                    js = slice(jb * half, (jb + 1) * half)
                    gap = col - cumt[pl.ds(h, 1), js]
                    e = jnp.exp(jnp.minimum(gap, 0.0)) * inner[rows, js]
                    if jb == rb:
                        e = jnp.where(causal, e, 0.0)
                    d = dot(e.astype(BF16), mv[js])
                    total = d if total is None else total + d
            parts.append(total)
        intra = jnp.concatenate(parts, axis=0)
        skip_row = jnp.where(left_row, skip[ha], skip[hb])
        y = intra + jnp.exp(cup) * cs[:, cols] + skip_row * xp
        z = proj[:, pl.ds(pl.multiple_of(hx + hn + p * 128, 128), 128)].astype(F32)
        g = y * (z * sigmoid(z))
        gated[:, cols] = g
        sqs[...] = sqs[...] + g * g
        last = cup[T - 1 : T, :]
        tail = (moved_f * jnp.exp(last - cup)).astype(BF16)
        add = dot_tn(tail, bv)
        for k, h in ((0, ha), (1, hb)):
            e = jnp.exp(cumcol[h, T - 1 : T, :])
            e = jnp.concatenate([e, e], axis=1)
            final[h] = e * state[h] + add[k * MP : (k + 1) * MP]
        return carry

    lax.fori_loop(0, heads // 2, pair, 0)
    col = jnp.sum(sqs[...], axis=-1, keepdims=True)
    rows = jnp.broadcast_to(col, (T, 128)).T
    sq_out[...] = rows[0:8]


def project_call(tok, gain, cos, sin, wdt, bias, decay, convw, hist, skip, state, weights):
    heads = state.shape[0]
    hx = heads * MP
    hn = 2 * MN
    hq = weights[0].shape[1]
    width = tok.shape[1]
    total = hq + 2 * HEAD + 2 * hx + hn
    vm = pl.BlockSpec(memory_space=pltpu.VMEM)
    hbm = pl.BlockSpec(memory_space=pl.ANY)
    sm = pl.BlockSpec(memory_space=pltpu.SMEM)
    return pl.pallas_call(
        project_kernel,
        out_shape=(
            jax.ShapeDtypeStruct((T // CH, (hq // HEAD) * CH, HEAD), BF16),
            jax.ShapeDtypeStruct((T, HEAD), BF16),
            jax.ShapeDtypeStruct((T, HEAD), BF16),
            jax.ShapeDtypeStruct((T, hx), F32),
            jax.ShapeDtypeStruct((8, T), F32),
            jax.ShapeDtypeStruct((heads, MP, MN), F32),
        ),
        in_specs=[vm] * 9 + [sm, vm] + [hbm] * 6,
        out_specs=[vm] * 6,
        scratch_shapes=[
            pltpu.VMEM((width, total), BF16),
            pltpu.VMEM((T, width), BF16),
            pltpu.VMEM((T, 2 * hx + hn), BF16),
            pltpu.VMEM((T + 8, 128), F32),
            pltpu.VMEM((T, hx + hn), BF16),
            pltpu.VMEM((T, T), F32),
            pltpu.VMEM((T, hx), F32),
            pltpu.VMEM((128, T), F32),
            pltpu.VMEM((heads, T, 128), F32),
            pltpu.VMEM((heads, T, 128), F32),
            pltpu.VMEM((T, 128), F32),
            pltpu.SemaphoreType.DMA((6,)),
        ],
        compiler_params=pltpu.CompilerParams(vmem_limit_bytes=56 * 1024 * 1024),
        cost_estimate=pl.CostEstimate(
            flops=20_000_000_000, bytes_accessed=60_000_000, transcendentals=5_000_000
        ),
        name="project_mamba",
    )(tok, gain, cos, sin, wdt, bias, decay, convw, hist, skip, state, *weights)


def attend_kernel(
    owner, length, q, k_new, v_new, gated, sq, mgain, pages, wa, wm,
    out,
    kc, vc, scores, ssm, wav, wmv, ny, sq_peer, own, send, recv, ctx, sems, ssems, rsems,
):
    tp = lax.axis_index("tp")
    peer = {"tp": 1 - tp}
    cps = []
    for i, (src, dst) in enumerate(((wm, wmv), (wa, wav))):
        cp = pltpu.make_async_copy(src, dst, sems.at[i])
        cp.start()
        cps.append(cp)
    barrier = pltpu.get_barrier_semaphore()
    pl.semaphore_signal(barrier, inc=1, device_id=peer, device_id_type=MESH)
    pl.semaphore_wait(barrier, 1)
    sq_copy = pltpu.make_async_remote_copy(
        src_ref=sq, dst_ref=sq_peer, send_sem=ssems.at[4], recv_sem=rsems.at[4],
        device_id=peer, device_id_type=MESH,
    )
    sq_copy.start()
    npages = owner.shape[0]

    def compact(i, carry):
        o = owner[i]
        rows = pl.ds(pl.multiple_of(i * 128, 128), 128)
        kc[rows, :] = pages[o, 0]
        vc[rows, :] = pages[o, 1]
        return carry

    lax.fori_loop(0, npages, compact, 0)
    cached = npages * 128
    kc[cached : cached + T, :] = k_new[...]
    vc[cached : cached + T, :] = v_new[...]
    sq_copy.wait()
    half = own.shape[1]
    hx = gated.shape[1]
    inv = lax.rsqrt((sq[0:1, :] + sq_peer[0:1, :]) * (1.0 / DSSM) + EPSILON)
    col = jnp.broadcast_to(inv, (128, T)).T

    def norm_tile(n, carry):
        cols = pl.ds(pl.multiple_of(n * 128, 128), 128)
        ny[:, cols] = (gated[:, cols] * col * mgain[:, cols]).astype(BF16)
        return carry

    lax.fori_loop(0, hx // 128, norm_tile, 0)
    cps[0].wait()

    def ssm_tile(n, carry):
        cols = pl.ds(pl.multiple_of(n * 256, 256), 256)
        ssm[:, cols] = dot(ny[...], wmv[:, cols])
        return carry

    lax.fori_loop(0, ssm.shape[1] // 256, ssm_tile, 0)
    cps[1].wait()
    heads = q.shape[1] // CH
    m_rows = heads * CH
    factor = 1.0 / math.sqrt(HEAD) * math.log2(math.e)
    kb = 512
    nblk = cached // kb
    safe = (cached * 3 // 4) // kb
    rows_i = lax.broadcasted_iota(jnp.int32, (m_rows, T), 0)
    cols_j = lax.broadcasted_iota(jnp.int32, (m_rows, T), 1)
    row_in = lax.rem(rows_i, CH)
    send_off = pl.multiple_of((1 - tp) * half, half)
    own_off = pl.multiple_of(tp * half, half)
    limit = length[0]

    def chunk_copy(c):
        return pltpu.make_async_remote_copy(
            src_ref=send.at[c], dst_ref=recv.at[c], send_sem=ssems.at[c], recv_sem=rsems.at[c],
            device_id=peer, device_id_type=MESH,
        )

    def chunk(c, carry):
        qc = q[c]
        top = jnp.full((m_rows, 128), NEG_FILL, F32)
        for b in range(nblk + 1):
            cols = slice(b * kb, (b + 1) * kb)
            s = dot_nt(qc, kc[cols, :])
            if b == nblk:
                s = jnp.where(cols_j <= row_in + c * CH, s, NEG_FILL)
            elif b >= safe:
                s = jnp.where(cols_j < limit - b * kb, s, NEG_FILL)
            scores[:, cols] = s
            for t in range(kb // 128):
                top = jnp.maximum(top, s[:, t * 128 : (t + 1) * 128])
        m = jnp.max(top, axis=-1, keepdims=True) * factor
        total = jnp.zeros((m_rows, 128), F32)
        acc = jnp.zeros((m_rows, HEAD), F32)
        for b in range(nblk + 1):
            cols = slice(b * kb, (b + 1) * kb)
            p = jnp.exp2(scores[:, cols] * factor - m)
            for t in range(kb // 128):
                total = total + p[:, t * 128 : (t + 1) * 128]
            acc = acc + dot(p.astype(BF16), vc[cols, :])
        res = (acc / jnp.sum(total, axis=-1, keepdims=True)).astype(BF16)
        for h in range(heads):
            ctx[:, h * HEAD : (h + 1) * HEAD] = res[h * CH : (h + 1) * CH]
        rows = pl.ds(pl.multiple_of(c * CH, CH), CH)
        cx = ctx[...]
        send[c] = (
            dot(cx, wav[:, pl.ds(send_off, half)]) + ssm[rows, pl.ds(send_off, half)]
        ).astype(BF16)
        own[rows, :] = dot(cx, wav[:, pl.ds(own_off, half)]) + ssm[rows, pl.ds(own_off, half)]
        chunk_copy(c).start()
        return carry

    lax.fori_loop(0, T // CH, chunk, 0)

    def finish(c, carry):
        rows = pl.ds(pl.multiple_of(c * CH, CH), CH)
        chunk_copy(c).wait()
        out[rows, :] = (own[rows, :] + recv[c].astype(F32)).astype(BF16)
        return carry

    lax.fori_loop(0, T // CH, finish, 0)


def attend_call(owner, length, q, k_new, v_new, gated, sq, mgain, pages, wa, wm):
    width = wa.shape[1]
    half = width // 2
    keys = owner.shape[0] * 128 + T
    chunks = T // CH
    hx = gated.shape[1]
    vm = pl.BlockSpec(memory_space=pltpu.VMEM)
    hbm = pl.BlockSpec(memory_space=pl.ANY)
    sm = pl.BlockSpec(memory_space=pltpu.SMEM)
    return pl.pallas_call(
        attend_kernel,
        out_shape=jax.ShapeDtypeStruct((T, half), BF16),
        in_specs=[sm, sm] + [vm] * 7 + [hbm, hbm],
        out_specs=vm,
        scratch_shapes=[
            pltpu.VMEM((keys, HEAD), BF16),
            pltpu.VMEM((keys, HEAD), BF16),
            pltpu.VMEM((q.shape[1], keys), F32),
            pltpu.VMEM((T, width), F32),
            pltpu.VMEM(wa.shape, BF16),
            pltpu.VMEM(wm.shape, BF16),
            pltpu.VMEM((T, hx), BF16),
            pltpu.VMEM((8, T), F32),
            pltpu.VMEM((T, half), F32),
            pltpu.VMEM((chunks, CH, half), BF16),
            pltpu.VMEM((chunks, CH, half), BF16),
            pltpu.VMEM((CH, wa.shape[0]), BF16),
            pltpu.SemaphoreType.DMA((2,)),
            pltpu.SemaphoreType.DMA((chunks + 1,)),
            pltpu.SemaphoreType.DMA((chunks + 1,)),
        ],
        compiler_params=pltpu.CompilerParams(
            collective_id=0, has_side_effects=True, vmem_limit_bytes=58 * 1024 * 1024
        ),
        name="attend_out",
    )(owner, length, q, k_new, v_new, gated, sq, mgain, pages, wa, wm)


def shards(
    tokens, attn_gain, w_query, key_weight, value_weight, w_attn_out, kv_pages, page_table,
    cached_len, w_gate_z, w_ssm_in, w_bc, w_dt, conv_w_x, conv_w_bc, conv_x_state, conv_bc_state,
    dt_bias, decay_rate, skip_gain, mixer_gain, w_mixer_out, ssm_state,
):
    devices = lax.axis_size("req")
    pages_dev = kv_pages.shape[0]
    row = page_table[0]
    owner = row // pages_dev
    slot = row % pages_dev
    targets = jnp.arange(devices, dtype=jnp.int32)
    want = jnp.sum(jnp.where(owner[None, :] == targets[:, None], slot[None, :], 0), axis=1)
    gathered = lax.all_gather(tokens, "tp", axis=1, tiled=True)
    requested = lax.all_to_all(want, "req", split_axis=0, concat_axis=0, tiled=True)
    fetched = kv_pages[:, :, 0][requested]
    arrived = lax.all_to_all(fetched, "req", split_axis=0, concat_axis=0, tiled=True)

    half = HEAD // 2
    inverse = ROPE_BASE ** (-2.0 * jnp.arange(half, dtype=F32) / HEAD)
    positions = cached_len[0] + jnp.arange(T, dtype=jnp.int32)
    angles = positions.astype(F32)[:, None] * inverse[None, :]
    c, s = jnp.cos(angles), jnp.sin(angles)
    cos = jnp.concatenate([c, c], axis=-1)
    sin = jnp.concatenate([-s, s], axis=-1)
    heads = w_dt.shape[1]
    wdt = jnp.pad(w_dt, ((0, 0), (0, 128 - heads)))
    bias = jnp.pad(dt_bias, (0, 128 - heads))[None]
    decay = jnp.pad(decay_rate, (0, 128 - heads))[None]
    convw = jnp.concatenate([conv_w_x, conv_w_bc], axis=1)
    hist = jnp.concatenate([conv_x_state[0], conv_bc_state[0]], axis=1).astype(F32)
    hist = jnp.pad(hist, ((5, 0), (0, 0)))
    q, k_new, v_new, gated, sq, final = project_call(
        gathered, attn_gain[None], cos, sin, wdt, bias, decay, convw, hist, skip_gain,
        ssm_state[0], (w_query, key_weight, value_weight, w_ssm_in, w_bc, w_gate_z),
    )
    mixed = attend_call(
        owner, cached_len, q, k_new, v_new, gated, sq, mixer_gain[None], arrived,
        w_attn_out, w_mixer_out,
    )
    return (mixed, final[None])


def solution(mesh):
    return jax.shard_map(
        shards,
        mesh=mesh,
        in_specs=(
            P("req", "tp"), P(), P(None, "tp"), P(None, "tp"), P(None, "tp"), P("tp", None),
            P("req", None, "tp", None, None), P("req", None), P("req"), P(None, "tp"),
            P(None, "tp"), P(), P(None, "tp"), P(None, "tp"), P(), P("req", None, "tp"),
            P("req", None, None), P("tp"), P("tp"), P("tp"), P("tp"), P("tp", None),
            P("req", "tp", None, None),
        ),
        out_specs=(P("req", "tp"), P("req", "tp", None, None)),
        check_vma=False,
    )
```

time: 271 us -> 189 us (0.70); the launches traced: 267 us -> 188 us
  matrix products: 101 us -> 0 us
  Pallas kernels: 0 us -> 67.5 us
  other arithmetic: 61.1 us -> 5.85 us
  waiting for transfers between devices: 35.4 us -> 62.5 us
  blocking collectives: 3.78 us -> 21.4 us
  local copies, waits for them, and re-layouts: 26.9 us -> 9.99 us
  starting transfers between devices: 22.2 us -> 6.04 us
    dot_general x21 -> x0, matrix products: 101 us -> none  [the longest x4 41.1 us: attend(): jnp.dot(weights.astype(jnp.bfloat16), value_rows, preferred_element_type=...]
    pallas_call x0 -> x2, Pallas kernels: none -> 67.5 us  [the longest x1 44.2 us: attend_call(): pl.pallas_call(attend_kernel, out_shape=jax.ShapeDtypeStruct((T, half), B...]
    all_gather x1, waiting for transfers between devices: 0.35 us -> 62 us  [shards(): gathered = lax.all_gather(tokens, 'tp', axis=1, tiled=True)]
    reduce_scatter x1 -> x0, waiting for transfers between devices: 33 us -> none  [shards(): lax.psum_scatter((attn_part + ssm_part).astype(jnp.bfloat16), 'tp', scatt...]
    reduce_sum x8 -> x1, other arithmetic: 27.7 us -> 0.09 us  [shards(): jnp.sum(jnp.where(owner[None, :] == targets[:, None], slot[None, :], 0),...]
    all_to_all x0 -> x1, blocking collectives: none -> 21.4 us  [shards(): lax.all_to_all(want, 'req', split_axis=0, concat_axis=0, tiled=True)]
    concatenate x4 -> x2, other arithmetic: 14.6 us -> 1.63 us  [the longest x1 1.03 us: shards(): cos = jnp.concatenate([c, c], axis=-1)]
    all_to_all x1 -> x0, starting transfers between devices: 12.3 us -> none  [shards(): lax.all_to_all(want_slot, 'req', split_axis=0, concat_axis=0, tiled=True)]
  transfers between devices with their start and end apart: 4 -> 2, of which waited for: 3 -> 1; matrix products, arithmetic and copies ran while one was open for 29% -> 3% of each run, Pallas kernels for 0% -> 12%
where the time goes in v1:
time: 189 us; the launch traced here: 188 us
  Pallas kernels  67.5 us (36%)
  waiting for transfers between devices  62.5 us (33%)
  blocking collectives  21.4 us (11%)
  between operations  14.8 us (8%)
  local copies, waits for them, and re-layouts  9.99 us (5%)
  starting transfers between devices  6.04 us (3%)
  other arithmetic  5.85 us (3%)
    all_gather x1, waiting for transfers between devices, shards(): gathered = lax.all_gather(tokens, 'tp', axis=1, tiled=True)  62 us
    pallas_call x1, Pallas kernels, attend_call(): pl.pallas_call(attend_kernel, out_shape=jax.ShapeDtypeStruct((T, half), B...  44.2 us
    pallas_call x1, Pallas kernels, project_call(): pl.pallas_call(project_kernel, out_shape=(jax.ShapeDtypeStruct((T // CH,...  23.3 us
    all_to_all x1, blocking collectives, shards(): lax.all_to_all(want, 'req', split_axis=0, concat_axis=0, tiled=True)  21.4 us
    all_to_all x1, starting transfers between devices, shards(): lax.all_to_all(fetched, 'req', split_axis=0, concat_axis=0, tiled=True)  5.82 us
    gather x1, local copies, waits for them, and re-layouts, shards(): fetched = kv_pages[:, :, 0][requested]  5.25 us
  transfers between devices with their start and end apart: 2, of which 1 were waited for; matrix products, arithmetic and copies ran while one was open for 3% of the time, Pallas kernels for 12%

profile of v1, /device:TPU:1, one launch (start us, length us, event | category | flops | bytes accessed | tf_op | source)
XLA Modules:
  0.0 188.0 jit_solution(8677213136071512126)
XLA Ops:
  7.2 0.7 fusion.7
  7.8 0.1 select_reduce_fusion
  7.9 0.1 copy.31
  8.0 21.4 %all_to_all.17 = s32[64,1,1]{2,1,0:T(1,128)S(1)} all-to-all(s32[64,1,1]{2,1,0:T(1,128)S(1)} %copy.31), channel_id=1, replica_groups=mesh['req'=64,'tp'=2] {'req'}, dimensions={0} | all-to-all | bytes 512 | tf_op jit(solution)/shard_map/all_to_all | solution.py:408
  29.4 1.2 reduce
  30.7 5.2 %gather_fusion = bf16[64,2,128,128]{3,2,1,0:T(8,128)(2,1)} fusion(bf16[64,2,128,128]{3,2,1,0:T(8,128)(2,1)} %bitcast.29, s32[1024]{0:T(1024)S(1)} %pad_clamp_fusion), kind=kCustom, calls=%fused_computation | custom fusion | bytes 8388864 | tf_op jit(solution)/shard_map/gather | solution.py:409
  35.9 0.0 copy-start
  35.9 0.0 copy-start.5
  35.9 0.0 copy-start.6
  35.9 0.0 copy-start.7
  35.9 5.8 %all-to-all-start.1 = ((bf16[64,2,128,128]{3,2,1,0:T(8,128)(2,1)}), bf16[64,2,128,128]{3,2,1,0:T(8,128)(2,1)}, u32[]{:S(2)}, u32[]{:S(2)}) async-start(bf16[64,2,128,128]{3,2,1,0:T(8,128)(2,1)} %gather_fusion), calls=%async_computation.1 | async-start | bytes 8388608 | tf_op jit(solution)/shard_map/all_to_all | solution.py:410
  41.8 0.0 copy-start.8
  41.8 0.0 copy-start.1
  41.8 0.0 copy-start.2
  41.8 0.0 copy-start.3
  41.8 0.0 copy-start.4
  41.8 0.2 all-gather.2.cloned.1.call-start
  42.0 0.5 all-gather.2.cloned.1.call-update
  43.2 0.0 copy-done
  43.2 0.3 copy.30
  43.5 0.0 copy-done.5
  43.5 0.6 broadcast_in_dim.38.mgain
  44.1 0.9 pad.17.wdt
  45.0 0.0 copy-done.6
  45.0 0.0 copy-done.7
  45.0 0.5 pad_bitcast_fusion
  45.6 1.0 fusion
  46.6 1.0 pad_maximum_fusion
  47.6 0.0 copy-done.8
  47.6 0.6 and_select_fusion.2.owner
  48.2 0.0 copy-done.1
  48.2 0.0 copy-done.2
  48.2 0.6 pad_maximum_fusion.2.convw
  48.8 0.0 copy-done.3
  48.8 0.0 copy-done.4
  48.8 0.6 fusion.4.hist
  49.5 62.0 %all-gather.2.cloned.1.call-done.tok = bf16[512,2048]{1,0:T(8,128)(2,1)} async-done(((bf16[512,1024]{1,0:T(8,128)(2,1)}), bf16[512,2048]{1,0:T(8,128)(2,1)}) %all-gather.2.cloned.1.call-update) | async-done | bytes 2097168 | tf_op jit(solution)/shard_map/all_gather | solution.py:407
  111.4 23.3 %project_mamba.1 = (bf16[4,512,128]{2,1,0:T(8,128)(2,1)}, bf16[512,128]{1,0:T(8,128)(2,1)}, bf16[512,128]{1,0:T(8,128)(2,1)}, f32[512,768]{1,0:T(8,128)}, f32[8,512]{1,0:T(8,128)}, /*index=5*/f32[12,64,256]{2,1,0:T(8,128)}) custom-call(bf16[512,2048]{1,0:T(8,128)(2,1)} %all-gather.2.cloned.1.call-done.tok, f32[1,2048]{1,0:T(1,128)} %bitcast.34, ...), custom_call_target="tpu_custom_call" | custom-call | flops 20000000000 | bytes 60000000 | tf_op jit(solution)/shard_map/project_mamba/pallas_call | solution.py:205
  134.7 0.0 all-to-all-done.1.pages
  134.7 44.2 %attend_out.1 = bf16[512,1024]{1,0:T(8,128)(2,1)} custom-call(s32[32]{0:T(128)} %and_select_fusion.2.owner, s32[1]{0:T(128)} %copy.33.length, bf16[4,512,128]{2,1,0:T(8,128)(2,1)} %get-tuple-element.8.q, bf16[512,128]{1,0:T(8,128)(2,1)} %get-tuple-element.9.k_new, bf16[512,128]{1,0:T(8,128)(2,1)} %get-tuple-element.10.v_new, ...), custom_call_target="tpu_custom_call" | custom-call | tf_op jit(solution)/shard_map/attend_out/pallas_call | solution.py:366
  178.9 2.3 %copy.34 = bf16[512,1024]{1,0:T(8,128)(2,1)} copy(bf16[512,1024]{1,0:T(8,128)(2,1)} %attend_out.1) | data formatting | bytes 2097152
  (4 shorter events, 0.0 us)
Async XLA Ops:
  35.9 7.3 %copy-start = (bf16[2048,12]{0,1:T(8,128)(2,1)S(1)}, bf16[2048,12]{0,1:T(8,128)(2,1)}, u32[]{:S(2)}) copy-start(bf16[2048,12]{0,1:T(8,128)(2,1)} %param.35) | copy-start | bytes 147460
  35.9 7.6 %copy-start.5 = (f32[768]{0:T(1024)S(1)}, f32[768]{0:T(1024)}, u32[]{:S(2)}) copy-start(f32[768]{0:T(1024)} %param.43) | copy-start | bytes 9220
  35.9 9.1 %copy-start.6 = (f32[12]{0:T(128)S(1)}, f32[12]{0:T(128)}, u32[]{:S(2)}) copy-start(f32[12]{0:T(128)} %param.41) | copy-start | bytes 148
  35.9 9.1 %copy-start.7 = (f32[12]{0:T(128)S(1)}, f32[12]{0:T(128)}, u32[]{:S(2)}) copy-start(f32[12]{0:T(128)} %param.40) | copy-start | bytes 148
  35.9 98.8 %all-to-all-start.1 = ((bf16[64,2,128,128]{3,2,1,0:T(8,128)(2,1)}), bf16[64,2,128,128]{3,2,1,0:T(8,128)(2,1)}, u32[]{:S(2)}, u32[]{:S(2)}) async-start(bf16[64,2,128,128]{3,2,1,0:T(8,128)(2,1)} %gather_fusion), calls=%async_computation.1 | async-start | bytes 8388608 | tf_op jit(solution)/shard_map/all_to_all | solution.py:410
  41.8 5.9 %copy-start.8 = (s32[1,32]{1,0:T(1,128)S(1)}, s32[1,32]{1,0:T(1,128)}, u32[]{:S(2)}) copy-start(s32[1,32]{1,0:T(1,128)} %param.30) | copy-start | bytes 388
  41.8 6.4 %copy-start.1 = (f32[4,768]{1,0:T(4,128)S(1)}, f32[4,768]{1,0:T(4,128)}, u32[]{:S(2)}) copy-start(f32[4,768]{1,0:T(4,128)} %param.36) | copy-start | bytes 36868
  41.8 6.4 %copy-start.2 = (f32[4,512]{1,0:T(4,128)S(1)}, f32[4,512]{1,0:T(4,128)}, u32[]{:S(2)}) copy-start(f32[4,512]{1,0:T(4,128)} %param.37) | copy-start | bytes 24580
  41.8 7.0 %copy-start.3 = (bf16[1,3,768]{2,1,0:T(4,128)(2,1)S(1)}, bf16[1,3,768]{2,1,0:T(4,128)(2,1)}, u32[]{:S(2)}) copy-start(bf16[1,3,768]{2,1,0:T(4,128)(2,1)} %param.38) | copy-start | bytes 13828
  41.8 7.0 %copy-start.4 = (bf16[1,3,512]{2,1,0:T(4,128)(2,1)S(1)}, bf16[1,3,512]{2,1,0:T(4,128)(2,1)}, u32[]{:S(2)}) copy-start(bf16[1,3,512]{2,1,0:T(4,128)(2,1)} %param.39) | copy-start | bytes 9220
  41.8 69.6 %all-gather.2.cloned.1.call-start = ((), (), s32[]{:S(2)}) async-start(), calls=%async_computation.2 | async-start | bytes 3145728 | tf_op jit(solution)/shard_map/all_gather | solution.py:407
Sparse Core Ops, SparseCore 0:
  44.3 67.0 all-gather.1

commit v2 on v1

--- a/solution.py
+++ b/solution.py
@@ -47,40 +47,161 @@
 
 
 def project_kernel(
-    tok, gain, cos, sin, wdt, bias, decay, convw, hist, skip, state,
-    wq, wk, wv, wx, wbc, wz,
-    q_out, k_out, v_out, gated, sq_out, final,
-    w, normed, proj, ub, xbc, inner, cs, cumt, cumcol, stepcol, sqs, sems,
+    table, tok, length, gain, bias, decay, skip, wdt, convx, convbc, histx, histbc, state,
+    pages, wq, wk, wv, wx, wbc, wz,
+    q_out, k_out, v_out, gated, sq_out, final, kc, vc,
+    w, tokf, normed, proj, ub, xbc, inner, cs, cumt, cumcol, stepcol, sqs, wdtv, cos, sin,
+    want, wants, wants_sm, kvl, sendbuf, arr,
+    sems, tsend, trecv, wsend, wrecv, psend, precv,
 ):
+    me = lax.axis_index("req")
+    tp = lax.axis_index("tp")
+    ndev = kvl.shape[0] if kvl.shape[0] == wants.shape[0] else wants.shape[0]
     hq, hx, hn = wq.shape[1], wx.shape[1], wbc.shape[1]
-    offs = [0, hq, hq + HEAD]
+    half = tok.shape[1]
+    heads = skip.shape[0]
     base = hq + 2 * HEAD
-    offs += [base, base + hx, base + hx + hn]
+    offs = [0, hq, hq + HEAD, base, base + hx, base + hx + hn]
+    kv_copy = pltpu.make_async_copy(pages.at[:, :, 0], kvl, sems.at[6])
+    kv_copy.start()
     copies = []
     for i, (src, off) in enumerate(zip((wq, wk, wv, wx, wbc, wz), offs)):
         cp = pltpu.make_async_copy(src, w.at[:, pl.ds(off, src.shape[1])], sems.at[i])
         cp.start()
         copies.append(cp)
-
-    def norm_rows(i, carry):
-        rows = pl.ds(pl.multiple_of(i * 64, 64), 64)
-        v = tok[rows, :].astype(F32)
-        mean_sq = jnp.mean(v * v, axis=-1, keepdims=True)
-        normed[rows, :] = (v * lax.rsqrt(mean_sq + EPSILON) * gain[...]).astype(BF16)
-        return carry
-
-    lax.fori_loop(0, T // 64, norm_rows, 0)
-
-    step_raw = dot(normed[...], wdt[...])
-    v = step_raw + bias[...]
+    tok_own = pltpu.make_async_copy(tok, tokf.at[tp], sems.at[7])
+    tok_own.start()
+
+    barrier = pltpu.get_barrier_semaphore()
+
+    def greet(i, carry):
+        pl.semaphore_signal(
+            barrier, inc=1, device_id={"req": lax.rem(me + i, ndev)}, device_id_type=MESH
+        )
+        return carry
+
+    pl.semaphore_signal(barrier, inc=1, device_id={"tp": 1 - tp}, device_id_type=MESH)
+    lax.fori_loop(1, ndev, greet, 0)
+
+    per_dev = kvl.shape[0]
+    npages = table.shape[1]
+    lanes = lax.broadcasted_iota(jnp.int32, want.shape, 1)
+    row = jnp.zeros(want.shape, jnp.int32)
+    for p in range(npages):
+        entry = table[0, p]
+        hit = lanes == lax.div(entry, per_dev)
+        row = jnp.where(hit, lax.rem(entry, per_dev), row)
+    want[...] = row
+    wants[pl.ds(me, 1)] = row[None]
+    pl.semaphore_wait(barrier, ndev)
+
+    def tok_copy(c):
+        rows = pl.ds(pl.multiple_of(c * CH, CH), CH)
+        return pltpu.make_async_remote_copy(
+            src_ref=tok.at[rows, :], dst_ref=tokf.at[tp, rows, :],
+            send_sem=tsend.at[c], recv_sem=trecv.at[c],
+            device_id={"tp": 1 - tp}, device_id_type=MESH,
+        )
+
+    def want_copy(i, slot, target):
+        return pltpu.make_async_remote_copy(
+            src_ref=want, dst_ref=wants.at[slot], send_sem=wsend.at[i], recv_sem=wrecv.at[slot],
+            device_id={"req": target}, device_id_type=MESH,
+        )
+
+    def want_start(i, carry):
+        want_copy(i, me, lax.rem(me + i, ndev)).start()
+        return carry
+
+    lax.fori_loop(1, ndev, want_start, 0)
+    for c in range(T // CH):
+        tok_copy(c).start()
+
+    def want_wait(i, carry):
+        o = lax.rem(me + i, ndev)
+        cp = want_copy(i, o, o)
+        cp.wait_send()
+        cp.wait_recv()
+        return carry
+
+    lax.fori_loop(1, ndev, want_wait, 0)
+    to_smem = pltpu.make_async_copy(wants, wants_sm, sems.at[8])
+    to_smem.start()
+    to_smem.wait()
+    kv_copy.wait()
+
+    def reader(t):
+        y = lax.rem(me // 16 + (t // 8) % 4, 4)
+        zh = lax.rem((me // 8) % 2 + t // 32, 2)
+        x = lax.rem((me // 2) % 4 + (t // 2) % 4, 4)
+        c = lax.rem(me % 2 + t % 2, 2)
+        return ((y * 2 + zh) * 4 + x) * 2 + c
+
+    def page_copy(t, slot, target):
+        return pltpu.make_async_remote_copy(
+            src_ref=sendbuf.at[t], dst_ref=arr.at[slot], send_sem=psend.at[t],
+            recv_sem=precv.at[slot], device_id={"req": target}, device_id_type=MESH,
+        )
+
+    arr[pl.ds(me, 1)] = kvl[pl.ds(wants_sm[me, 0, me], 1)]
+
+    def page_pack(t, carry):
+        sendbuf[pl.ds(t, 1)] = kvl[pl.ds(wants_sm[reader(t), 0, me], 1)]
+        return carry
+
+    def page_start(t, carry):
+        page_copy(t, me, reader(t)).start()
+        return carry
+
+    lax.fori_loop(1, ndev, page_pack, 0)
+    lax.fori_loop(1, ndev, page_start, 0)
+
+    lane = lax.broadcasted_iota(jnp.int32, (T, HEAD), 1)
+    freq = jnp.exp(lax.rem(lane, HEAD // 2).astype(F32) * (-2.0 * math.log(ROPE_BASE) / HEAD))
+    posn = (length[0] + lax.broadcasted_iota(jnp.int32, (T, HEAD), 0)).astype(F32)
+    angle = posn * freq
+    cos[...] = jnp.cos(angle)
+    sn = jnp.sin(angle)
+    sin[...] = jnp.where(lane < HEAD // 2, -sn, sn)
+    wdtv[...] = jnp.zeros_like(wdtv)
+    wdtv[0:heads, :] = wdt[...]
+    head_lane = lax.broadcasted_iota(jnp.int32, (1, 128), 1)
+    bias_row = jnp.zeros((1, 128), F32)
+    decay_row = jnp.zeros((1, 128), F32)
+    for h in range(heads):
+        bias_row = jnp.where(head_lane == h, bias[h], bias_row)
+        decay_row = jnp.where(head_lane == h, decay[h], decay_row)
+
+    tok_own.wait()
+    for c in range(T // CH):
+        cp = pltpu.make_async_remote_copy(
+            src_ref=tok.at[c * CH : (c + 1) * CH, :],
+            dst_ref=tokf.at[1 - tp, c * CH : (c + 1) * CH, :],
+            send_sem=tsend.at[c], recv_sem=trecv.at[c],
+            device_id={"tp": 1 - tp}, device_id_type=MESH,
+        )
+        cp.wait_recv()
+
+        def norm_rows(i, carry):
+            rows = pl.ds(pl.multiple_of(c * CH + i * 64, 64), 64)
+            v0 = tokf[0, rows, :].astype(F32)
+            v1 = tokf[1, rows, :].astype(F32)
+            ms = jnp.sum(v0 * v0, axis=-1, keepdims=True) + jnp.sum(v1 * v1, axis=-1, keepdims=True)
+            scale = lax.rsqrt(ms * (0.5 / half) + EPSILON)
+            normed[rows, 0:half] = (v0 * scale * gain[:, 0:half]).astype(BF16)
+            normed[rows, half:] = (v1 * scale * gain[:, half:]).astype(BF16)
+            return carry
+
+        lax.fori_loop(0, CH // 64, norm_rows, 0)
+
+    v = dot_nt(normed[...], wdtv[...]) + bias_row
     step = jnp.maximum(v, 0.0) + jnp.log1p(jnp.exp(-jnp.abs(v)))
     ri = lax.broadcasted_iota(jnp.int32, (T, T), 0)
     ci = lax.broadcasted_iota(jnp.int32, (T, T), 1)
     tri = jnp.where(ri >= ci, 1.0, 0.0).astype(BF16)
-    hi, mid, low = split3(-step * decay[...])
+    hi, mid, low = split3(-step * decay_row)
     cum = dot(tri, hi) + (dot(tri, mid) + dot(tri, low))
     cumt[...] = cum.T
-    heads = skip.shape[0]
     for h in range(heads):
         cumcol[h] = jnp.broadcast_to(cum[:, h : h + 1], (T, 128))
         stepcol[h] = jnp.broadcast_to(step[:, h : h + 1], (T, 128))
@@ -111,11 +232,12 @@
     nconv = (hx + hn) // 256
     lax.fori_loop(0, nconv, proj_tile, 0)
 
-    def conv_tile(n, carry):
-        cols = pl.ds(pl.multiple_of(n * 128, 128), 128)
-        ub[0:8, :] = hist[:, cols]
+    def conv_tile(n, carry, hist, convw, start):
+        local = pl.ds(pl.multiple_of(n * 128, 128), 128)
+        cols = pl.ds(pl.multiple_of(start + n * 128, 128), 128)
+        ub[5:8, :] = hist[:, local].astype(F32)
         ub[8 : T + 8, :] = proj[:, cols].astype(F32)
-        taps = convw[:, cols]
+        taps = convw[:, local]
         s = ub[5 : T + 5, :] * taps[0:1]
         s = s + ub[6 : T + 6, :] * taps[1:2]
         s = s + ub[7 : T + 7, :] * taps[2:3]
@@ -123,7 +245,8 @@
         xbc[:, cols] = (s * sigmoid(s)).astype(BF16)
         return carry
 
-    lax.fori_loop(0, (hx + hn) // 128, conv_tile, 0)
+    lax.fori_loop(0, hx // 128, partial(conv_tile, hist=histx, convw=convx, start=0), 0)
+    lax.fori_loop(0, hn // 128, partial(conv_tile, hist=histbc, convw=convbc, start=hx), 0)
     copies[5].wait()
     lax.fori_loop(nconv, nconv + hx // 256, proj_tile, 0)
 
@@ -191,17 +314,42 @@
     rows = jnp.broadcast_to(col, (T, 128)).T
     sq_out[...] = rows[0:8]
 
-
-def project_call(tok, gain, cos, sin, wdt, bias, decay, convw, hist, skip, state, weights):
+    def page_wait(t, carry):
+        o = reader(t)
+        cp = page_copy(t, o, o)
+        cp.wait_recv()
+        cp.wait_send()
+        return carry
+
+    lax.fori_loop(1, ndev, page_wait, 0)
+
+    def compact(i, carry):
+        o = lax.div(table[0, i], per_dev)
+        rows = pl.ds(pl.multiple_of(i * 128, 128), 128)
+        kc[rows, :] = arr[o, 0]
+        vc[rows, :] = arr[o, 1]
+        return carry
+
+    lax.fori_loop(0, npages, compact, 0)
+    for c in range(T // CH):
+        tok_copy(c).wait_send()
+
+
+def project_call(ndev, table, tok, length, gain, bias, decay, skip, wdt, convx, convbc, histx, histbc,
+                 state, pages, weights):
     heads = state.shape[0]
     hx = heads * MP
     hn = 2 * MN
     hq = weights[0].shape[1]
-    width = tok.shape[1]
+    half = tok.shape[1]
+    width = 2 * half
     total = hq + 2 * HEAD + 2 * hx + hn
+    cached = table.shape[1] * 128
+    per_dev = pages.shape[0]
     vm = pl.BlockSpec(memory_space=pltpu.VMEM)
     hbm = pl.BlockSpec(memory_space=pl.ANY)
     sm = pl.BlockSpec(memory_space=pltpu.SMEM)
+    dma = pltpu.SemaphoreType.DMA
     return pl.pallas_call(
         project_kernel,
         out_shape=(
@@ -211,11 +359,14 @@
             jax.ShapeDtypeStruct((T, hx), F32),
             jax.ShapeDtypeStruct((8, T), F32),
             jax.ShapeDtypeStruct((heads, MP, MN), F32),
+            jax.ShapeDtypeStruct((cached, HEAD), BF16),
+            jax.ShapeDtypeStruct((cached, HEAD), BF16),
         ),
-        in_specs=[vm] * 9 + [sm, vm] + [hbm] * 6,
-        out_specs=[vm] * 6,
+        in_specs=[sm, vm, sm, vm, sm, sm, sm] + [vm] * 6 + [hbm] * 7,
+        out_specs=[vm] * 8,
         scratch_shapes=[
             pltpu.VMEM((width, total), BF16),
+            pltpu.VMEM((2, T, half), BF16),
             pltpu.VMEM((T, width), BF16),
             pltpu.VMEM((T, 2 * hx + hn), BF16),
             pltpu.VMEM((T + 8, 128), F32),
@@ -226,18 +377,32 @@
             pltpu.VMEM((heads, T, 128), F32),
             pltpu.VMEM((heads, T, 128), F32),
             pltpu.VMEM((T, 128), F32),
-            pltpu.SemaphoreType.DMA((6,)),
+            pltpu.VMEM((128, width), BF16),
+            pltpu.VMEM((T, HEAD), F32),
+            pltpu.VMEM((T, HEAD), F32),
+            pltpu.VMEM((1, 128), jnp.int32),
+            pltpu.VMEM((ndev, 1, 128), jnp.int32),
+            pltpu.SMEM((ndev, 1, 128), jnp.int32),
+            pltpu.VMEM((per_dev, 2, 128, HEAD), BF16),
+            pltpu.VMEM((ndev, 2, 128, HEAD), BF16),
+            pltpu.VMEM((ndev, 2, 128, HEAD), BF16),
+            dma((9,)),
+            dma((T // CH,)),
+            dma((T // CH,)),
+            dma((ndev,)),
+            dma((ndev,)),
+            dma((ndev,)),
+            dma((ndev,)),
         ],
-        compiler_params=pltpu.CompilerParams(vmem_limit_bytes=56 * 1024 * 1024),
-        cost_estimate=pl.CostEstimate(
-            flops=20_000_000_000, bytes_accessed=60_000_000, transcendentals=5_000_000
+        compiler_params=pltpu.CompilerParams(
+            collective_id=1, has_side_effects=True, vmem_limit_bytes=63 * 1024 * 1024
         ),
-        name="project_mamba",
-    )(tok, gain, cos, sin, wdt, bias, decay, convw, hist, skip, state, *weights)
+        name="gather_project",
+    )(table, tok, length, gain, bias, decay, skip, wdt, convx, convbc, histx, histbc, state, pages, *weights)
 
 
 def attend_kernel(
-    owner, length, q, k_new, v_new, gated, sq, mgain, pages, wa, wm,
+    length, q, k_new, v_new, gated, sq, mgain, kc_in, vc_in, wa, wm,
     out,
     kc, vc, scores, ssm, wav, wmv, ny, sq_peer, own, send, recv, ctx, sems, ssems, rsems,
 ):
@@ -256,17 +421,9 @@
         device_id=peer, device_id_type=MESH,
     )
     sq_copy.start()
-    npages = owner.shape[0]
-
-    def compact(i, carry):
-        o = owner[i]
-        rows = pl.ds(pl.multiple_of(i * 128, 128), 128)
-        kc[rows, :] = pages[o, 0]
-        vc[rows, :] = pages[o, 1]
-        return carry
-
-    lax.fori_loop(0, npages, compact, 0)
-    cached = npages * 128
+    cached = kc_in.shape[0]
+    kc[0:cached, :] = kc_in[...]
+    vc[0:cached, :] = vc_in[...]
     kc[cached : cached + T, :] = k_new[...]
     vc[cached : cached + T, :] = v_new[...]
     sq_copy.wait()
@@ -354,10 +511,10 @@
     lax.fori_loop(0, T // CH, finish, 0)
 
 
-def attend_call(owner, length, q, k_new, v_new, gated, sq, mgain, pages, wa, wm):
+def attend_call(length, q, k_new, v_new, gated, sq, mgain, kc, vc, wa, wm):
     width = wa.shape[1]
     half = width // 2
-    keys = owner.shape[0] * 128 + T
+    keys = kc.shape[0] + T
     chunks = T // CH
     hx = gated.shape[1]
     vm = pl.BlockSpec(memory_space=pltpu.VMEM)
@@ -366,7 +523,7 @@
     return pl.pallas_call(
         attend_kernel,
         out_shape=jax.ShapeDtypeStruct((T, half), BF16),
-        in_specs=[sm, sm] + [vm] * 7 + [hbm, hbm],
+        in_specs=[sm] + [vm] * 8 + [hbm, hbm],
         out_specs=vm,
         scratch_shapes=[
             pltpu.VMEM((keys, HEAD), BF16),
@@ -389,7 +546,7 @@
             collective_id=0, has_side_effects=True, vmem_limit_bytes=58 * 1024 * 1024
         ),
         name="attend_out",
-    )(owner, length, q, k_new, v_new, gated, sq, mgain, pages, wa, wm)
+    )(length, q, k_new, v_new, gated, sq, mgain, kc, vc, wa, wm)
 
 
 def shards(
@@ -397,39 +554,14 @@
     cached_len, w_gate_z, w_ssm_in, w_bc, w_dt, conv_w_x, conv_w_bc, conv_x_state, conv_bc_state,
     dt_bias, decay_rate, skip_gain, mixer_gain, w_mixer_out, ssm_state,
 ):
-    devices = lax.axis_size("req")
-    pages_dev = kv_pages.shape[0]
-    row = page_table[0]
-    owner = row // pages_dev
-    slot = row % pages_dev
-    targets = jnp.arange(devices, dtype=jnp.int32)
-    want = jnp.sum(jnp.where(owner[None, :] == targets[:, None], slot[None, :], 0), axis=1)
-    gathered = lax.all_gather(tokens, "tp", axis=1, tiled=True)
-    requested = lax.all_to_all(want, "req", split_axis=0, concat_axis=0, tiled=True)
-    fetched = kv_pages[:, :, 0][requested]
-    arrived = lax.all_to_all(fetched, "req", split_axis=0, concat_axis=0, tiled=True)
-
-    half = HEAD // 2
-    inverse = ROPE_BASE ** (-2.0 * jnp.arange(half, dtype=F32) / HEAD)
-    positions = cached_len[0] + jnp.arange(T, dtype=jnp.int32)
-    angles = positions.astype(F32)[:, None] * inverse[None, :]
-    c, s = jnp.cos(angles), jnp.sin(angles)
-    cos = jnp.concatenate([c, c], axis=-1)
-    sin = jnp.concatenate([-s, s], axis=-1)
-    heads = w_dt.shape[1]
-    wdt = jnp.pad(w_dt, ((0, 0), (0, 128 - heads)))
-    bias = jnp.pad(dt_bias, (0, 128 - heads))[None]
-    decay = jnp.pad(decay_rate, (0, 128 - heads))[None]
-    convw = jnp.concatenate([conv_w_x, conv_w_bc], axis=1)
-    hist = jnp.concatenate([conv_x_state[0], conv_bc_state[0]], axis=1).astype(F32)
-    hist = jnp.pad(hist, ((5, 0), (0, 0)))
-    q, k_new, v_new, gated, sq, final = project_call(
-        gathered, attn_gain[None], cos, sin, wdt, bias, decay, convw, hist, skip_gain,
-        ssm_state[0], (w_query, key_weight, value_weight, w_ssm_in, w_bc, w_gate_z),
+    ndev = lax.axis_size("req")
+    q, k_new, v_new, gated, sq, final, kc, vc = project_call(
+        ndev, page_table, tokens, cached_len, attn_gain[None], dt_bias, decay_rate, skip_gain,
+        w_dt.T, conv_w_x, conv_w_bc, conv_x_state[0], conv_bc_state[0], ssm_state[0], kv_pages,
+        (w_query, key_weight, value_weight, w_ssm_in, w_bc, w_gate_z),
     )
     mixed = attend_call(
-        owner, cached_len, q, k_new, v_new, gated, sq, mixer_gain[None], arrived,
-        w_attn_out, w_mixer_out,
+        cached_len, q, k_new, v_new, gated, sq, mixer_gain[None], kc, vc, w_attn_out, w_mixer_out,
     )
     return (mixed, final[None])
 

time: 189 us -> 147 us (0.78)
  Pallas kernels: 67.5 us -> 141 us
  waiting for transfers between devices: 62.5 us -> 0 us
  blocking collectives: 21.4 us -> 0 us
  between operations: 14.8 us -> 1.3 us
  starting transfers between devices: 6.04 us -> 0 us
  other arithmetic: 5.85 us -> 0 us
  local copies, waits for them, and re-layouts: 9.99 us -> 4.41 us
    pallas_call x1, Pallas kernels: 23.3 us -> 97 us  [project_call(): pl.pallas_call(project_kernel, out_shape=(jax.ShapeDtypeStruct((T // CH,...]
    all_gather x1 -> x0, waiting for transfers between devices: 62 us -> none  [shards(): gathered = lax.all_gather(tokens, 'tp', axis=1, tiled=True)]
    all_to_all x1 -> x0, blocking collectives: 21.4 us -> none  [shards(): lax.all_to_all(want, 'req', split_axis=0, concat_axis=0, tiled=True)]
    all_to_all x1 -> x0, starting transfers between devices: 5.82 us -> none  [shards(): lax.all_to_all(fetched, 'req', split_axis=0, concat_axis=0, tiled=True)]
    gather x1 -> x0, local copies, waits for them, and re-layouts: 5.25 us -> none  [shards(): fetched = kv_pages[:, :, 0][requested]]
  transfers between devices with their start and end apart: 2 -> 0, of which waited for: 1 -> 0; matrix products, arithmetic and copies ran while one was open for 3% -> 0% of each run, Pallas kernels for 12% -> 0%
where the time goes in v2:
time: 147 us
  Pallas kernels  141 us (96%)
  local copies, waits for them, and re-layouts  4.41 us (3%)
    pallas_call x1, Pallas kernels, project_call(): pl.pallas_call(project_kernel, out_shape=(jax.ShapeDtypeStruct((T // CH,...  97 us
    pallas_call x1, Pallas kernels, attend_call(): pl.pallas_call(attend_kernel, out_shape=jax.ShapeDtypeStruct((T, half), B...  44.1 us
    unnamed x4, local copies, waits for them, and re-layouts  3.15 us

profile of v2, /device:TPU:1, one launch (start us, length us, event | category | flops | bytes accessed | tf_op | source)
XLA Modules:
  0.0 146.8 jit_solution(11783466935520534120)
XLA Ops:
  1.3 1.3 broadcast_in_dim.10.mgain
  2.5 97.0 %gather_project.1 = (bf16[4,512,128]{2,1,0:T(8,128)(2,1)}, bf16[512,128]{1,0:T(8,128)(2,1)}, bf16[512,128]{1,0:T(8,128)(2,1)}, f32[512,768]{1,0:T(8,128)}, f32[8...) custom-call(s32[1,32]{1,0:T(1,128)} %table.1, ...), custom_call_target="tpu_custom_call" | custom-call | tf_op jit(solution)/shard_map/gather_project/pallas_call | solution.py:353
  99.6 0.0 copy-start
  99.6 44.1 %attend_out.1 = bf16[512,1024]{1,0:T(8,128)(2,1)} custom-call(s32[1]{0:T(128)S(6)} %copy.27.length, bf16[4,512,128]{2,1,0:T(8,128)(2,1)} %get-tuple-element.10.q, bf16[512,128]{1,0:T(8,128)(2,1)} %get-tuple-element.11.k_new, bf16[512,128]{1,0:T(8,128)(2,1)} %get-tuple-element.12.v_new, f32[512,768]{1,0:T(8,128)} %get-tuple-element.13.gated, ...), custom_call_target="tpu_custom_call" | custom-call | tf_op jit(solution)/shard_map/attend_out/pallas_call | solution.py:523
  143.7 2.3 %copy.28 = bf16[512,1024]{1,0:T(8,128)(2,1)} copy(bf16[512,1024]{1,0:T(8,128)(2,1)} %attend_out.1) | data formatting | bytes 2097152
  145.9 0.0 copy-done
  145.9 0.9 copy.29
Async XLA Ops:
  99.6 46.4 %copy-start = (f32[12,64,256]{2,1,0:T(8,128)S(1)}, f32[12,64,256]{2,1,0:T(8,128)}, u32[]{:S(2)}) copy-start(f32[12,64,256]{2,1,0:T(8,128)} %get-tuple-element.17) | copy-start | bytes 2359300
